TPU v7x, 256 devices: a whole 4x4x8 slice. The times are simulated.
256 devices in a mesh: slab: 8 (over z), tile: 16 (over y, x), ch: 2 (over core).
Axes of the slice: x: 4, y: 4, z: 8, core: 2. Of those that a mesh axis runs over, the one named last changes fastest.
Arguments:
- volume: bfloat16 [16, 256, 1024], P('slab', 'tile'), may hold values from -6 to 6
- xz_tissue: int32 [256], P('tile'), may hold values 0 or 1
- yz_tissue: int32 [1024], P(('slab', 'tile')), may hold values 0 or 1
- first_conv: bfloat16 [32, 9, 1], replicated, may hold values from -2 to 2
- second_conv: bfloat16 [32, 9, 32], replicated, may hold values from -0.375 to 0.375
- third_conv: bfloat16 [64, 9, 32], replicated, may hold values from -0.375 to 0.375
- fourth_conv: bfloat16 [64, 9, 64], replicated, may hold values from -0.25 to 0.25
- fifth_conv: bfloat16 [32, 9, 96], replicated, may hold values from -0.21875 to 0.21875
- sixth_conv: bfloat16 [32, 9, 32], replicated, may hold values from -0.375 to 0.375
- out_weight: bfloat16 [32], replicated, may hold values from -1 to 1
Outputs:
- restored: bfloat16 [16, 256, 1024], P('slab', 'tile')
All inputs are finite; a program needn't handle non-finite values. No bound on the sum of `xz_tissue` or of `yz_tissue` on one device may be relied on, other than what follows from the above.
Results may differ from a plain program's by a relative error of at most 0.0037.
Values may be sent and summed in bfloat16 or wider, within the bound.
No kernel may reach another device: no remote copies, remote signals or barrier semaphores. Data moves between devices by JAX's collectives and lax.ppermute only.
A program may use at most 128 MiB of HBM per device.

v0:
```python
import jax
import jax.numpy as jnp
from jax import lax
from jax.experimental import pallas as pl
from jax.experimental.pallas import tpu as pltpu
from jax.sharding import PartitionSpec as P

BF = jnp.bfloat16
F32 = jnp.float32
HALO = 8


def iota(shape, dim):
    return lax.broadcasted_iota(jnp.int32, shape, dim)


def dot(a, b):
    return jnp.dot(a, b, preferred_element_type=F32)


def spread(tap, cells):
    outs = tap.shape[1]
    shape = (outs, cells * outs)
    pick = (iota(shape, 0) == iota(shape, 1) % outs).astype(F32).astype(BF)
    return dot(tap, pick)


def stack_rows(tap, cells):
    return jnp.concatenate([tap] * cells, axis=0)


def prep_kernel(w1, w2, w3, w4, w5, w6, wo, t1, t2, t3, t4, t5, t6, th):
    def fine(src, dst, lo, hi, base):
        row, lane = iota((256, 256), 0) // 32, iota((256, 256), 1) // 32
        g = [spread(src[t, lo:hi, :], 8) for t in range(9)]
        edge = iota((32, 256), 1) // 32
        for s in range(3):
            tile = jnp.zeros((256, 256), F32)
            for r in range(3):
                tile = jnp.where(row == lane + (r - 1), stack_rows(g[3 * r + s], 8), tile)
            tile = tile.astype(BF)
            below = jnp.where(edge == 7, g[6 + s], 0.0).astype(BF)
            above = jnp.where(edge == 0, g[s], 0.0).astype(BF)
            for d in dst:
                d[0, 256 * s : 256 * s + 256, :] = tile
                d[1, 256 * s : 256 * s + 256, :] = tile
                d[0, base + 32 * s : base + 32 * s + 32, :] = below
                d[1, base + 32 * s : base + 32 * s + 32, :] = above

    fine(w2, [t2], 0, 32, 768)
    fine(w6, [t6], 0, 32, 768)
    fine(w5, [t5.at[0], t5.at[1]], 64, 96, 1280)

    row, lane = iota((16, 256), 0), iota((16, 256), 1) // 32
    for s in range(3):
        g = [spread(w1[3 * r + s, :, :], 8) for r in range(3)]
        for h in range(2):
            tile = jnp.zeros((16, 256), F32)
            for r in range(3):
                tile = jnp.where(row == lane + 8 * h + (r - 1), jnp.broadcast_to(g[r][0:1], (16, 256)), tile)
            t1[h, 16 * s : 16 * s + 16, :] = tile.astype(BF)

    row, lane = iota((256, 256), 0) // 32, iota((256, 256), 1) // 64
    g = [spread(w3[t, :, :], 4) for t in range(9)]
    for s in range(3):
        for h in range(2):
            tile = jnp.zeros((256, 256), F32)
            for r in range(3):
                tile = jnp.where(row == lane + 4 * h + (r - 1), stack_rows(g[3 * r + s], 8), tile)
            t3[h, 256 * s : 256 * s + 256, :] = tile.astype(BF)

    row, lane = iota((256, 256), 0) // 64, iota((256, 256), 1) // 64
    edge = iota((64, 256), 1) // 64
    g = [spread(w4[t, :, :], 4) for t in range(9)]
    for s in range(3):
        tile = jnp.zeros((256, 256), F32)
        for r in range(3):
            tile = jnp.where(row == lane + (r - 1), stack_rows(g[3 * r + s], 4), tile)
        tile = tile.astype(BF)
        for h in range(2):
            t4[h, 256 * s : 256 * s + 256, :] = tile
        t4[0, 768 + 64 * s : 832 + 64 * s, :] = jnp.where(edge == 3, g[6 + s], 0.0).astype(BF)
        t4[1, 768 + 64 * s : 832 + 64 * s, :] = jnp.where(edge == 0, g[s], 0.0).astype(BF)

    row, lane = iota((256, 256), 0) // 64, iota((256, 256), 1) // 32
    edge = iota((64, 256), 1) // 32
    g = [spread(w5[t, 0:64, :], 8) for t in range(9)]
    for q in range(2):
        groups = ((0,), (1, 2)) if q == 0 else ((0, 1), (2,))
        for i, taps in enumerate(groups):
            tile = jnp.zeros((256, 256), F32)
            for r in range(3):
                part = sum(g[3 * r + s] for s in taps)
                hit = row == ((lane + (r - 1) + 2) // 2 - 1)
                tile = tile + jnp.where(hit, stack_rows(part, 4), 0.0)
            tile = tile.astype(BF)
            for h in range(2):
                t5[q, h, 768 + 256 * i : 1024 + 256 * i, :] = tile
            below = sum(g[6 + s] for s in taps)
            above = sum(g[s] for s in taps)
            t5[q, 0, 1376 + 64 * i : 1440 + 64 * i, :] = jnp.where(edge == 7, below, 0.0).astype(BF)
            t5[q, 1, 1376 + 64 * i : 1440 + 64 * i, :] = jnp.where(edge == 0, above, 0.0).astype(BF)

    row, lane = iota((512, 128), 0), iota((512, 128), 1)
    pick = (iota((512, 32), 0) % 32 == iota((512, 32), 1)).astype(F32).astype(BF)
    column = dot(pick, wo[...])
    th[...] = jnp.where(row // 32 == lane, column, 0.0).astype(BF)


def prepare(w1, w2, w3, w4, w5, w6, wo):
    taps = [jnp.transpose(w, (1, 2, 0)) for w in (w1, w2, w3, w4, w5, w6)]
    head = jnp.broadcast_to(wo[:, None], (wo.shape[0], 128))
    shapes = [(2, 48, 256), (2, 864, 256), (2, 768, 256), (2, 960, 256), (2, 2, 1504, 256), (2, 864, 256), (512, 128)]
    return pl.pallas_call(
        prep_kernel,
        out_shape=[jax.ShapeDtypeStruct(s, BF) for s in shapes],
        cost_estimate=pl.CostEstimate(flops=400_000_000, bytes_accessed=5_000_000, transcendentals=0),
        name="prep",
    )(*taps, head)


def network(edges, n, wh, p, l1, a1, a2, pool, m1, m2, d1, weights, emit):
    t1, t2, t3, t4, t5, t6, th = weights
    pairs = wh + 8

    def rows(j, off, size):
        return pl.ds(pl.multiple_of((j + 4) * n + off, 16), size)

    def loop(count, cols, body):
        size = cols * n
        if count == cols:
            body(0, 0, size)
            return

        def step(i, carry):
            body(i * cols, i * size, size)
            return carry

        lax.fori_loop(0, count // cols, step, 0)

    def clear(ref, lead, first):
        for at in lead:
            for side, j, num in ((0, -first, first), (1, wh, first)):

                @pl.when(edges[side] > 0)
                def _(at=at, j=j, num=num):
                    ref[at + (rows(j, 0, num * n), slice(None))] = jnp.zeros((num * n, ref.shape[-1]), ref.dtype)

    both = [(0,), (1,)]
    four = [(q, h) for q in range(2) for h in range(2)]

    def near(q):
        return ((1, -1), (0, 0), (1, 0)) if q == 0 else ((0, 0), (1, 0), (0, 1))

    clear(p, both, 4)
    for q in range(2):
        j0 = -3 if q == 0 else -4
        size = (wh + 7) * n
        for s, (qs, dj) in enumerate(near(q)):
            l1[q, rows(j0, 0, size), 16 * s : 16 * s + 16] = p[qs, rows(j0 + dj, 0, size), :]

    def relu(v):
        return jnp.maximum(v, 0.0).astype(BF)

    c1 = {15: 5, 39: 13}[wh + 7]
    for q in range(2):
        j0 = -3 if q == 0 else -4

        def body(dj, off, size, q=q, j0=j0):
            r = rows(j0, off, size)
            x = l1[q, r, 0:48]
            for h in range(2):
                a1[q, h, r, :] = relu(dot(x, t1[h]))

        loop(wh + 7, c1, body)
    clear(a1, four, 4)

    def fine_inputs(src, q, h, j0, off, size):
        other = slice(0, 32) if h == 0 else slice(224, 256)
        own = [src[qs, h, rows(j0 + dj, off, size), :] for qs, dj in near(q)]
        edge = [src[qs, 1 - h, rows(j0 + dj, off, size), other] for qs, dj in near(q)]
        return own, edge

    c2 = (wh + 6) // 2
    for q, h in four:

        def body(dj, off, size, q=q, h=h):
            own, edge = fine_inputs(a1, q, h, -3, off, size)
            a2[q, h, rows(-3, off, size), :] = relu(dot(jnp.concatenate(own + edge, axis=1), t2[h]))

        loop(wh + 6, c2, body)
    clear(a2, four, 3)

    def pick_pool():
        shape = (1024, 256)
        row, lane = iota(shape, 0), iota(shape, 1)
        cell = 4 * (row // 512) + ((row // 32) % 8) // 2
        return jnp.where((cell == lane // 32) & (row % 32 == lane % 32), 0.25, 0.0).astype(BF)

    pm = pick_pool()

    def body(dj, off, size):
        r = rows(-3, off, size)
        x = jnp.concatenate([a2[0, 0, r, :], a2[1, 0, r, :], a2[0, 1, r, :], a2[1, 1, r, :]], axis=1)
        pool[r, :] = dot(x, pm).astype(BF)

    loop(wh + 6, c2, body)

    c3 = (wh + 4) // 2

    def body(dj, off, size):
        x = jnp.concatenate([pool[rows(-2 + k, off, size), :] for k in (-1, 0, 1)], axis=1)
        for h in range(2):
            m1[h, rows(-2, off, size), :] = relu(dot(x, t3[h]))

    loop(wh + 4, c3, body)
    clear(m1, both, 2)

    c4 = (wh + 2) // 2
    for h in range(2):

        def body(dj, off, size, h=h):
            other = slice(0, 64) if h == 0 else slice(192, 256)
            own = [m1[h, rows(-1 + k, off, size), :] for k in (-1, 0, 1)]
            edge = [m1[1 - h, rows(-1 + k, off, size), other] for k in (-1, 0, 1)]
            m2[h, rows(-1, off, size), :] = relu(dot(jnp.concatenate(own + edge, axis=1), t4[h]))

        loop(wh + 2, c4, body)
    clear(m2, both, 1)

    c5 = {9: 3, 33: 11}[wh + 1]
    for q, h in four:
        j0 = 0 if q == 0 else -1

        def body(dj, off, size, q=q, h=h, j0=j0):
            own, edge = fine_inputs(a2, q, h, j0, off, size)
            other = slice(0, 64) if h == 0 else slice(192, 256)
            cells = (-1, 0) if q == 0 else (0, 1)
            own += [m2[h, rows(j0 + k, off, size), :] for k in cells]
            edge += [m2[1 - h, rows(j0 + k, off, size), other] for k in cells]
            d1[q, h, rows(j0, off, size), :] = relu(dot(jnp.concatenate(own + edge, axis=1), t5[q, h]))

        loop(wh + 1, c5, body)
    clear(d1, four, 1)

    c6 = wh // 2
    for q in range(2):

        def body(dj, off, size, q=q):
            parts = []
            for h in range(2):
                own, edge = fine_inputs(d1, q, h, 0, off, size)
                parts.append(relu(dot(jnp.concatenate(own + edge, axis=1), t6[h])))
            emit(q, dj, c6, dot(jnp.concatenate(parts, axis=1), th[...]))

        loop(wh, c6, body)


def unet_scratch(n, wh):
    m = (wh + 8) * n
    return [
        pltpu.VMEM((2, m, 16), BF),
        pltpu.VMEM((2, m, 128), BF),
        pltpu.VMEM((2, 2, m, 256), BF),
        pltpu.VMEM((2, 2, m, 256), BF),
        pltpu.VMEM((m, 256), BF),
        pltpu.VMEM((2, m, 256), BF),
        pltpu.VMEM((2, m, 256), BF),
        pltpu.VMEM((2, 2, m, 256), BF),
    ]


def xz_kernel(edges, v, *refs):
    weights, (out, vf, pf, hx), scratch = refs[:7], refs[7:11], refs[11:]
    n, wh = 16, 32
    for z in range(16):
        vf[16 * z : 16 * z + 16, :] = v[z].astype(F32)
    for y in range(16):
        turned = jnp.transpose(vf[pl.ds(y, 16, stride=16), :])
        pf[pl.ds(y, 80, stride=16), 0:16] = turned[0:80, :]
    p = scratch[0]
    for x in range(80):
        p[x % 2, 16 * (x // 2) : 16 * (x // 2) + 16, :] = pf[16 * x : 16 * x + 16, 0:16].astype(BF)

    def emit(q, j0, cols, head):
        for k in range(cols):
            at = pl.multiple_of((2 * (j0 + k) + q) * n, 16)
            hx[pl.ds(at, n), :] = head[k * n : k * n + n, :]

    network(edges, n, wh, *scratch, weights, emit)
    for y in range(16):
        out[y] = jnp.transpose(hx[pl.ds(y, 64, stride=16), :])[0:16, :]


def yz_kernel(edges, xflags, v, before, after, yflags, xz, *refs):
    weights, (out, vf, hf, hy, rf), scratch = refs[:7], refs[7:12], refs[12:]
    n, wh = 64, 8
    p = scratch[0]
    for z in range(16):
        vf[16 * z : 16 * z + 16, :] = v[z].astype(F32)
        hf[16 * z : 16 * z + 8, :] = before[z, 8:16, :].astype(F32)
        hf[16 * z + 8 : 16 * z + 16, :] = after[z, 0:8, :].astype(F32)
    for k in range(32):
        if k < 8:
            plane = hf[pl.ds(k, 16, stride=16), :]
        elif k < 24:
            plane = vf[pl.ds(k - 8, 16, stride=16), :]
        else:
            plane = hf[pl.ds(k - 16, 16, stride=16), :]
        turned = jnp.transpose(plane)
        p[k % 2, n * (k // 2) : n * (k // 2) + n, :] = turned[HALO : HALO + n, :].astype(BF)

    def emit(q, j0, cols, head):
        for k in range(cols):
            at = pl.multiple_of((2 * (j0 + k) + q) * n, 16)
            hy[pl.ds(at, n), :] = head[k * n : k * n + n, :]

    network(edges, n, wh, *scratch, weights, emit)

    yes = yflags[...] > 0
    for y in range(16):
        plane = pltpu.roll(vf[pl.ds(y, 16, stride=16), :], 128 - HALO, 1)[:, 0:64]
        yz = jnp.transpose(hy[64 * y : 64 * y + 64, :])[0:16, :]
        yz = jnp.where(yes, plane + yz, plane).astype(BF).astype(F32)
        xz_new = (plane + xz[y]).astype(BF).astype(F32)
        xz_new = jnp.where(xflags[y] > 0, xz_new, plane)
        rf[pl.ds(y, 16, stride=16), 0:64] = 0.5 * (xz_new + yz)
    for z in range(16):
        block = rf[16 * z : 16 * z + 16, 0:64].astype(BF)
        out[2 * (z // 2), z % 2] = block
        out[2 * (z // 2) + 1, z % 2] = block


def pack_kernel(side, v, out):
    for c, shift in ((0, HALO), (1, 1024 + HALO - 64)):

        @pl.when(side[0] == c)
        def _(shift=shift):
            for z in range(2):
                rolled = pltpu.roll(v[z].astype(F32), shift, 1).astype(BF)
                for s in range(8):
                    out[s, z] = rolled[:, 128 * s : 128 * s + 128]


SMEM = pl.BlockSpec(memory_space=pltpu.SMEM)
VMEM = pl.BlockSpec(memory_space=pltpu.VMEM)


def per_device(volume, xz_tissue, yz_tissue, *weights):
    slab, tile, ch = lax.axis_index("slab"), lax.axis_index("tile"), lax.axis_index("ch")
    packed = pl.pallas_call(
        pack_kernel,
        out_shape=jax.ShapeDtypeStruct((8, 2, 16, 128), BF),
        in_specs=[SMEM, VMEM],
        out_specs=VMEM,
        name="pack",
    )(ch[None].astype(jnp.int32), volume)
    moved = lax.all_to_all(packed, "slab", split_axis=0, concat_axis=0, tiled=True)
    v = moved.reshape(16, 16, 128)
    tables = prepare(*weights)

    flags = yz_tissue
    for bit in (1, 2, 4, 8):
        other = lax.ppermute(flags, "tile", [(i, i ^ bit) for i in range(16)])
        high = (tile & bit) > 0
        flags = jnp.where(high, jnp.concatenate([other, flags]), jnp.concatenate([flags, other]))
    yflags = lax.dynamic_slice_in_dim(flags, 64 * ch, 64, 0)[None, :]

    before = lax.ppermute(v, "tile", [(i, i + 1) for i in range(15)])
    after = lax.ppermute(v, "tile", [(i + 1, i) for i in range(15)])

    window = 2 * slab + ch
    xz_edges = jnp.stack([window == 0, window == 15]).astype(jnp.int32)
    yz_edges = jnp.stack([tile == 0, tile == 15]).astype(jnp.int32)

    xz = pl.pallas_call(
        xz_kernel,
        out_shape=jax.ShapeDtypeStruct((16, 16, 64), F32),
        in_specs=[SMEM] + [VMEM] * 8,
        out_specs=VMEM,
        scratch_shapes=[pltpu.VMEM((256, 128), F32), pltpu.VMEM((1280, 128), F32), pltpu.VMEM((1024, 128), F32)]
        + unet_scratch(16, 32),
        cost_estimate=pl.CostEstimate(flops=6_000_000_000, bytes_accessed=6_000_000, transcendentals=0),
        name="xz",
    )(xz_edges, v, *tables)

    block = pl.pallas_call(
        yz_kernel,
        out_shape=jax.ShapeDtypeStruct((16, 2, 16, 64), BF),
        in_specs=[SMEM, SMEM] + [VMEM] * 12,
        out_specs=VMEM,
        scratch_shapes=[
            pltpu.VMEM((256, 128), F32),
            pltpu.VMEM((256, 128), F32),
            pltpu.VMEM((1024, 128), F32),
            pltpu.VMEM((256, 128), F32),
        ]
        + unet_scratch(64, 8),
        cost_estimate=pl.CostEstimate(flops=6_000_000_000, bytes_accessed=6_000_000, transcendentals=0),
        name="yz",
    )(yz_edges, xz_tissue, v, before, after, yflags, xz, *tables)

    back = lax.all_to_all(block, ("slab", "ch"), split_axis=0, concat_axis=0, tiled=True)
    return jnp.transpose(back, (1, 2, 0, 3)).reshape(2, 16, 1024)


def solution(mesh):
    return jax.shard_map(
        per_device,
        mesh=mesh,
        in_specs=(P("slab", "tile", None), P("tile"), P(("slab", "tile"))) + (P(),) * 7,
        out_specs=P("slab", "tile", None),
        check_vma=False,
    )
```

profile of v0, /device:TPU:9, one launch (start us, length us, event | category | flops | bytes accessed | tf_op | source)
XLA Modules:
  0.0 106.4 jit_solution(1034978669295589410)
XLA Ops:
  0.0 1.2 %collective-permute-start.2 = (s32[8]{0:T(128)}, s32[8]{0:T(128)S(1)}, u32[]{:S(2)}, u32[]{:S(2)}) collective-permute-start(s32[8]{0:T(128)} %param.12), channel_id=1, source_target_pairs={{0,2},{2,0},{4,6},{6,4},{8,10},{10,8},{12,14},{14,12},{16,18},{18,... | collective-permute-start | bytes 104 | tf_op jit(solution)/shard_map/ppermute | solution.py:364
  1.2 1.6 %pack.1 = bf16[8,2,16,128]{3,2,1,0:T(8,128)(2,1)} custom-call(s32[1]{0:T(128)} %bitcast.2.side, bf16[2,16,1024]{2,1,0:T(8,128)(2,1)} %v.1), custom_call_target="tpu_custom_call" | custom-call | tf_op jit(solution)/shard_map/pack/pallas_call | solution.py:351
  2.8 8.2 %all-to-all-start = ((bf16[8,2,16,128]{3,2,1,0:T(8,128)(2,1)}), bf16[8,2,16,128]{3,2,1,0:T(8,128)(2,1)S(1)}, u32[]{:S(2)}, u32[]{:S(2)}) async-start(bf16[8,2,16,128]{3,2,1,0:T(8,128)(2,1)} %pack.1), calls=%async_computation | async-start | bytes 131072 | tf_op jit(solution)/shard_map/all_to_all | solution.py:358
  11.0 1.7 %copy.19 = bf16[32,9,96]{0,2,1:T(8,128)(2,1)} copy(bf16[32,9,96]{2,0,1:T(8,128)(2,1)} %param.17) | data formatting | bytes 110592 | tf_op args[7]
  12.7 1.7 %copy.18 = bf16[64,9,64]{0,2,1:T(8,128)(2,1)} copy(bf16[64,9,64]{2,0,1:T(8,128)(2,1)} %param.16) | data formatting | bytes 147456 | tf_op args[6]
  14.3 1.6 %copy.20 = bf16[32,9,32]{0,2,1:T(8,128)(2,1)} copy(bf16[32,9,32]{2,0,1:T(8,128)(2,1)} %param.18) | data formatting | bytes 36864 | tf_op args[8]
  16.0 1.6 %copy.17 = bf16[32,9,32]{0,2,1:T(8,128)(2,1)} copy(bf16[32,9,32]{2,0,1:T(8,128)(2,1)} %param.14) | data formatting | bytes 36864 | tf_op args[4]
  17.6 1.3 %copy.23 = bf16[32,9,1]{0,2,1:T(2,128)(2,1)} copy(bf16[32,9,1]{0,1,2:T(8,128)(2,1)} %param.13) | data formatting | bytes 1152 | tf_op args[3]
  18.8 0.7 add_convert_fusion.1.edges
  19.5 0.6 add_convert_fusion.edges
  20.1 1.3 %broadcast_in_dim.14.wo = bf16[32,128]{1,0:T(8,128)(2,1)} broadcast(bf16[32]{0:T(256)(128)(2,1)} %param.19), dimensions={0} | broadcast | bytes 8256 | tf_op jit(solution)/shard_map/broadcast_in_dim | solution.py:112
  21.4 4.7 %prep.1 = (bf16[2,48,256]{2,1,0:T(8,128)(2,1)}, bf16[2,864,256]{2,1,0:T(8,128)(2,1)}, bf16[2,768,256]{2,1,0:T(8,128)(2,1)}, bf16[2,960,256]{2,1,0:T(8,128)(2,1)}...) custom-call(bf16[9,1,32]{2,1,0:T(2,128)(2,1)} %bitcast.28, ...), custom_call_target="tpu_custom_call" | custom-call | flops 400000000 | bytes 5000000 | tf_op jit(solution)/shard_map/prep/pallas_call | solution.py:114
  26.1 0.0 collective-permute-done.2
  26.1 0.8 broadcast_select_fusion
  26.9 2.5 %collective-permute-start.3 = (s32[16]{0:T(128)S(1)}, s32[16]{0:T(128)S(1)}, u32[]{:S(2)}, u32[]{:S(2)}) collective-permute-start(s32[16]{0:T(128)S(1)} %broadcast_select_fusion), channel_id=1, source_target_pairs={{0,4},{2,6},{4,0},{6,2},{8,12},{10,14},{12,8},{14,10},{16,20},{18,... | collective-permute-start | bytes 200 | tf_op jit(solution)/shard_map/ppermute | solution.py:364
  29.4 1.5 %collective-permute-done.3 = s32[16]{0:T(128)S(1)} collective-permute-done((s32[16]{0:T(128)S(1)}, s32[16]{0:T(128)S(1)}, u32[]{:S(2)}, u32[]{:S(2)}) %collective-permute-start.3) | collective-permute-done | bytes 96 | tf_op jit(solution)/shard_map/ppermute | solution.py:364
  30.8 0.1 broadcast_select_fusion.1
  30.9 0.2 collective-permute-start.4
  31.1 2.2 %collective-permute-done.4 = s32[32]{0:T(128)S(1)} collective-permute-done((s32[32]{0:T(128)S(1)}, s32[32]{0:T(128)S(1)}, u32[]{:S(2)}, u32[]{:S(2)}) %collective-permute-start.4) | collective-permute-done | bytes 160 | tf_op jit(solution)/shard_map/ppermute | solution.py:364
  33.4 0.1 broadcast_select_fusion.2
  33.4 2.0 %collective-permute-start.5 = (s32[64]{0:T(128)S(1)}, s32[64]{0:T(128)S(1)}, u32[]{:S(2)}, u32[]{:S(2)}) collective-permute-start(s32[64]{0:T(128)S(1)} %broadcast_select_fusion.2), channel_id=1, source_target_pairs={{0,16},{2,18},{4,20},{6,22},{8,24},{10,26},{12,28},{14,30},{16,0},... | collective-permute-start | bytes 776 | tf_op jit(solution)/shard_map/ppermute | solution.py:364
  35.5 1.9 %collective-permute-done.5 = s32[64]{0:T(128)S(1)} collective-permute-done((s32[64]{0:T(128)S(1)}, s32[64]{0:T(128)S(1)}, u32[]{:S(2)}, u32[]{:S(2)}) %collective-permute-start.5) | collective-permute-done | bytes 288 | tf_op jit(solution)/shard_map/ppermute | solution.py:364
  37.4 0.1 broadcast_select_fusion.3
  37.5 0.7 dynamic-slice_bitcast_fusion.yflags
  38.1 0.0 all-to-all-done
  38.1 0.0 copy-start
  38.1 2.2 %collective-permute-start = (bf16[16,16,128]{2,1,0:T(8,128)(2,1)S(1)}, bf16[16,16,128]{2,1,0:T(8,128)(2,1)S(1)}, u32[]{:S(2)}, u32[]{:S(2)}) collective-permute-start(bf16[16,16,128]{2,1,0:T(8,128)(2,1)S(1)} %bitcast.24), channel_id=1, source_target_pairs={{0,2},{2,4},{4,6},{6,8},{8,10},{10,12},{12,14},{14,16},{16,18},{18... | collective-permute-start | bytes 196616 | tf_op jit(solution)/shard_map/ppermute | solution.py:369
  40.3 5.2 %collective-permute-start.1 = (bf16[16,16,128]{2,1,0:T(8,128)(2,1)S(1)}, bf16[16,16,128]{2,1,0:T(8,128)(2,1)S(1)}, u32[]{:S(2)}, u32[]{:S(2)}) collective-permute-start(bf16[16,16,128]{2,1,0:T(8,128)(2,1)S(1)} %bitcast.25), channel_id=1, source_target_pairs={{2,0},{4,2},{6,4},{8,6},{10,8},{12,10},{14,12},{16,14},{18,16},{20... | collective-permute-start | bytes 196616 | tf_op jit(solution)/shard_map/ppermute | solution.py:370
  45.5 0.0 copy-done
  45.5 18.0 %xz.1 = f32[16,16,64]{2,1,0:T(8,128)} custom-call(s32[2]{0:T(128)} %add_convert_fusion.1.edges, bf16[16,16,128]{2,1,0:T(8,128)(2,1)} %bitcast.26, bf16[2,48,256]{2,1,0:T(8,128)(2,1)} %get-tuple-element.12.refs_0_, bf16[2,864,256]{2,1,0:T(8,128)(2,1)} %get-tuple-element.13.refs_1_, bf16[2,768,256]{2,1,0:T(8,128)(2,1)} %get-tuple-element.14.refs_2_, ...), custom_call_target="tpu_custom_call" | custom-call | flops 6000000000 | bytes 6000000 | tf_op jit(solution)/shard_map/xz/pallas_call | solution.py:376
  63.6 0.0 collective-permute-done.before
  63.6 0.0 copy-start.1
  63.6 0.0 collective-permute-done.1.after
  63.6 0.6 copy-done.1
  64.2 0.0 copy-start.2
  64.2 0.6 copy-done.2
  64.8 19.5 %yz.1 = bf16[16,2,16,64]{3,2,1,0:T(8,128)(2,1)} custom-call(s32[2]{0:T(128)} %add_convert_fusion.edges, s32[16]{0:T(128)} %xflags.1, bf16[16,16,128]{2,1,0:T(8,128)(2,1)} %bitcast.27, bf16[16,16,128]{2,1,0:T(8,128)(2,1)} %copy-done.1, bf16[16,16,128]{2,1,0:T(8,128)(2,1)} %copy-done.2, s32[1,64]{1,0:T(1,128)} %dynamic-slice_bitcast_fusion.yflags, ...), custom_call_target="tpu_custom_call" | custom-call | flops 6000000000 | bytes 6000000 | tf_op jit(solution)/shard_map/yz/pallas_call | solution.py:387
  84.4 1.0 reshape.9
  85.4 20.0 %all_to_all.10 = bf16[16,2,1024]{2,1,0:T(2,128)(2,1)S(1)} all-to-all(bf16[16,2,1024]{2,1,0:T(2,128)(2,1)S(1)} %reshape.9), channel_id=1, replica_groups=mesh['slab'=8,'tile'=16,'ch'=2] {'slab','ch'}, dimensions={0} | all-to-all | bytes 131072 | tf_op jit(solution)/shard_map/all_to_all | solution.py:403
  105.5 0.1 reshape.10
  105.6 0.1 copy.21
  105.7 0.8 reshape.8
Async XLA Ops:
  0.0 26.1 %collective-permute-start.2 = (s32[8]{0:T(128)}, s32[8]{0:T(128)S(1)}, u32[]{:S(2)}, u32[]{:S(2)}) collective-permute-start(s32[8]{0:T(128)} %param.12), channel_id=1, source_target_pairs={{0,2},{2,0},{4,6},{6,4},{8,10},{10,8},{12,14},{14,12},{16,18},{18,... | collective-permute-start | bytes 104 | tf_op jit(solution)/shard_map/ppermute | solution.py:364
  2.8 35.4 %all-to-all-start = ((bf16[8,2,16,128]{3,2,1,0:T(8,128)(2,1)}), bf16[8,2,16,128]{3,2,1,0:T(8,128)(2,1)S(1)}, u32[]{:S(2)}, u32[]{:S(2)}) async-start(bf16[8,2,16,128]{3,2,1,0:T(8,128)(2,1)} %pack.1), calls=%async_computation | async-start | bytes 131072 | tf_op jit(solution)/shard_map/all_to_all | solution.py:358
  26.9 3.9 %collective-permute-start.3 = (s32[16]{0:T(128)S(1)}, s32[16]{0:T(128)S(1)}, u32[]{:S(2)}, u32[]{:S(2)}) collective-permute-start(s32[16]{0:T(128)S(1)} %broadcast_select_fusion), channel_id=1, source_target_pairs={{0,4},{2,6},{4,0},{6,2},{8,12},{10,14},{12,8},{14,10},{16,20},{18,... | collective-permute-start | bytes 200 | tf_op jit(solution)/shard_map/ppermute | solution.py:364
  30.9 2.4 %collective-permute-start.4 = (s32[32]{0:T(128)S(1)}, s32[32]{0:T(128)S(1)}, u32[]{:S(2)}, u32[]{:S(2)}) collective-permute-start(s32[32]{0:T(128)S(1)} %broadcast_select_fusion.1), channel_id=1, source_target_pairs={{0,8},{2,10},{4,12},{6,14},{8,0},{10,2},{12,4},{14,6},{16,24},{18,... | collective-permute-start | bytes 392 | tf_op jit(solution)/shard_map/ppermute | solution.py:364
  33.4 3.9 %collective-permute-start.5 = (s32[64]{0:T(128)S(1)}, s32[64]{0:T(128)S(1)}, u32[]{:S(2)}, u32[]{:S(2)}) collective-permute-start(s32[64]{0:T(128)S(1)} %broadcast_select_fusion.2), channel_id=1, source_target_pairs={{0,16},{2,18},{4,20},{6,22},{8,24},{10,26},{12,28},{14,30},{16,0},... | collective-permute-start | bytes 776 | tf_op jit(solution)/shard_map/ppermute | solution.py:364
  38.1 7.4 %copy-start = (bf16[8,2,16,128]{3,2,1,0:T(8,128)(2,1)}, bf16[8,2,16,128]{3,2,1,0:T(8,128)(2,1)S(1)}, u32[]{:S(2)}) copy-start(bf16[8,2,16,128]{3,2,1,0:T(8,128)(2,1)S(1)} %all-to-all-done) | copy-start | bytes 196612
  38.1 25.4 %collective-permute-start = (bf16[16,16,128]{2,1,0:T(8,128)(2,1)S(1)}, bf16[16,16,128]{2,1,0:T(8,128)(2,1)S(1)}, u32[]{:S(2)}, u32[]{:S(2)}) collective-permute-start(bf16[16,16,128]{2,1,0:T(8,128)(2,1)S(1)} %bitcast.24), channel_id=1, source_target_pairs={{0,2},{2,4},{4,6},{6,8},{8,10},{10,12},{12,14},{14,16},{16,18},{18... | collective-permute-start | bytes 196616 | tf_op jit(solution)/shard_map/ppermute | solution.py:369
  40.3 23.3 %collective-permute-start.1 = (bf16[16,16,128]{2,1,0:T(8,128)(2,1)S(1)}, bf16[16,16,128]{2,1,0:T(8,128)(2,1)S(1)}, u32[]{:S(2)}, u32[]{:S(2)}) collective-permute-start(bf16[16,16,128]{2,1,0:T(8,128)(2,1)S(1)} %bitcast.25), channel_id=1, source_target_pairs={{2,0},{4,2},{6,4},{8,6},{10,8},{12,10},{14,12},{16,14},{18,16},{20... | collective-permute-start | bytes 196616 | tf_op jit(solution)/shard_map/ppermute | solution.py:370
  63.6 0.6 copy-start.1
  64.2 0.6 copy-start.2
where the time goes:
time: 107 us; the launch traced here: 106 us
  Pallas kernels  43.9 us (41%)
  starting transfers between devices  21.5 us (20%)
  blocking collectives  20 us (19%)
  local copies, waits for them, and re-layouts  13.1 us (12%)
  waiting for transfers between devices  5.64 us (5%)
  other arithmetic  2.24 us (2%)
    all_to_all x1, blocking collectives, per_device(): lax.all_to_all(block, ('slab', 'ch'), split_axis=0, concat_axis=0, tiled=...  20 us
    pallas_call x1, Pallas kernels, per_device(): pl.pallas_call(yz_kernel, out_shape=jax.ShapeDtypeStruct((16, 2, 16, 64),...  19.5 us
    pallas_call x1, Pallas kernels, per_device(): pl.pallas_call(xz_kernel, out_shape=jax.ShapeDtypeStruct((16, 16, 64), F3...  18 us
    unnamed x13, local copies, waits for them, and re-layouts  10.3 us
    all_to_all x1, starting transfers between devices, per_device(): lax.all_to_all(packed, 'slab', split_axis=0, concat_axis=0, tiled=True)  8.19 us
    ppermute x4, starting transfers between devices, per_device(): other = lax.ppermute(flags, 'tile', [(i, i ^ bit) for i in range(16)])  5.92 us
    ppermute x4, waiting for transfers between devices, per_device(): other = lax.ppermute(flags, 'tile', [(i, i ^ bit) for i in range(16)])  5.63 us
    ppermute x1, starting transfers between devices, per_device(): after = lax.ppermute(v, 'tile', [(i + 1, i) for i in range(15)])  5.23 us
  transfers between devices with their start and end apart: 7, of which 3 were waited for; matrix products, arithmetic and copies ran while one was open for 11% of the time, Pallas kernels for 23%

commit v1 on v0

--- a/solution.py
+++ b/solution.py
@@ -5,8 +5,11 @@
 from jax.experimental.pallas import tpu as pltpu
 from jax.sharding import PartitionSpec as P
 
+
 BF = jnp.bfloat16
 F32 = jnp.float32
+SMEM = pl.BlockSpec(memory_space=pltpu.SMEM)
+VMEM = pl.BlockSpec(memory_space=pltpu.VMEM)
 HALO = 8
 
 
@@ -18,21 +21,27 @@
     return jnp.dot(a, b, preferred_element_type=F32)
 
 
-def spread(tap, cells):
-    outs = tap.shape[1]
+def spread(tap, cells, out_first):
+    outs = tap.shape[0 if out_first else 1]
     shape = (outs, cells * outs)
     pick = (iota(shape, 0) == iota(shape, 1) % outs).astype(F32).astype(BF)
-    return dot(tap, pick)
+    dims = (((0 if out_first else 1,), (0,)), ((), ()))
+    return lax.dot_general(tap, pick, dims, preferred_element_type=F32)
 
 
 def stack_rows(tap, cells):
     return jnp.concatenate([tap] * cells, axis=0)
 
 
-def prep_kernel(w1, w2, w3, w4, w5, w6, wo, t1, t2, t3, t4, t5, t6, th):
+def build_tables(held, t1, t2, t3, t4, t5, t6, th):
+    def part(first, last):
+        return lambda t, lo, hi: held[t, first:last, lo:hi]
+
+    w2, w3, w4, w5, w6 = part(0, 32), part(32, 64), part(64, 128), part(128, 160), part(160, 192)
+
     def fine(src, dst, lo, hi, base):
         row, lane = iota((256, 256), 0) // 32, iota((256, 256), 1) // 32
-        g = [spread(src[t, lo:hi, :], 8) for t in range(9)]
+        g = [spread(src(t, lo, hi), 8, True) for t in range(9)]
         edge = iota((32, 256), 1) // 32
         for s in range(3):
             tile = jnp.zeros((256, 256), F32)
@@ -52,16 +61,17 @@
     fine(w5, [t5.at[0], t5.at[1]], 64, 96, 1280)
 
     row, lane = iota((16, 256), 0), iota((16, 256), 1) // 32
+    first = spread(held[9, 0:16, 0:32], 8, False)
     for s in range(3):
-        g = [spread(w1[3 * r + s, :, :], 8) for r in range(3)]
+        g = [first[3 * r + s : 3 * r + s + 1, :] for r in range(3)]
         for h in range(2):
             tile = jnp.zeros((16, 256), F32)
             for r in range(3):
-                tile = jnp.where(row == lane + 8 * h + (r - 1), jnp.broadcast_to(g[r][0:1], (16, 256)), tile)
+                tile = jnp.where(row == lane + 8 * h + (r - 1), jnp.broadcast_to(g[r], (16, 256)), tile)
             t1[h, 16 * s : 16 * s + 16, :] = tile.astype(BF)
 
     row, lane = iota((256, 256), 0) // 32, iota((256, 256), 1) // 64
-    g = [spread(w3[t, :, :], 4) for t in range(9)]
+    g = [spread(w3(t, 0, 64), 4, False) for t in range(9)]
     for s in range(3):
         for h in range(2):
             tile = jnp.zeros((256, 256), F32)
@@ -71,7 +81,7 @@
 
     row, lane = iota((256, 256), 0) // 64, iota((256, 256), 1) // 64
     edge = iota((64, 256), 1) // 64
-    g = [spread(w4[t, :, :], 4) for t in range(9)]
+    g = [spread(w4(t, 0, 64), 4, True) for t in range(9)]
     for s in range(3):
         tile = jnp.zeros((256, 256), F32)
         for r in range(3):
@@ -84,7 +94,7 @@
 
     row, lane = iota((256, 256), 0) // 64, iota((256, 256), 1) // 32
     edge = iota((64, 256), 1) // 32
-    g = [spread(w5[t, 0:64, :], 8) for t in range(9)]
+    g = [spread(w5(t, 0, 64), 8, True) for t in range(9)]
     for q in range(2):
         groups = ((0,), (1, 2)) if q == 0 else ((0, 1), (2,))
         for i, taps in enumerate(groups):
@@ -102,26 +112,44 @@
             t5[q, 1, 1376 + 64 * i : 1440 + 64 * i, :] = jnp.where(edge == 0, above, 0.0).astype(BF)
 
     row, lane = iota((512, 128), 0), iota((512, 128), 1)
-    pick = (iota((512, 32), 0) % 32 == iota((512, 32), 1)).astype(F32).astype(BF)
-    column = dot(pick, wo[...])
+    pick = (iota((512, 32), 0) % 32 == iota((512, 32), 1)).astype(F32)
+    column = jnp.sum(pick * held[9, 16:32, 0:32].astype(F32)[0:1], axis=1, keepdims=True)
     th[...] = jnp.where(row // 32 == lane, column, 0.0).astype(BF)
 
 
+def stage_kernel(w1, w2, w3, w4, w5, w6, wo, out):
+    for t in range(9):
+        out[t, 0:32, 0:32] = w2[t]
+        out[t, 32:64, 0:64] = w3[t]
+        out[t, 64:128, 0:64] = w4[t]
+        out[t, 128:160, 0:96] = w5[t]
+        out[t, 160:192, 0:32] = w6[t]
+    out[9, 0:32, :] = jnp.zeros((32, 128), BF)
+    out[9, 0:9, 0:32] = w1[...]
+    out[9, 16:17, 0:32] = wo[...]
+
+
+def stage(raw):
+    return pl.pallas_call(
+        stage_kernel,
+        out_shape=jax.ShapeDtypeStruct((10, 192, 128), BF),
+        in_specs=[VMEM] * 7,
+        out_specs=VMEM,
+        name="stage",
+    )(*raw)
+
+
 def prepare(w1, w2, w3, w4, w5, w6, wo):
-    taps = [jnp.transpose(w, (1, 2, 0)) for w in (w1, w2, w3, w4, w5, w6)]
-    head = jnp.broadcast_to(wo[:, None], (wo.shape[0], 128))
-    shapes = [(2, 48, 256), (2, 864, 256), (2, 768, 256), (2, 960, 256), (2, 2, 1504, 256), (2, 864, 256), (512, 128)]
-    return pl.pallas_call(
-        prep_kernel,
-        out_shape=[jax.ShapeDtypeStruct(s, BF) for s in shapes],
-        cost_estimate=pl.CostEstimate(flops=400_000_000, bytes_accessed=5_000_000, transcendentals=0),
-        name="prep",
-    )(*taps, head)
+    taps = [jnp.transpose(w1[:, :, 0])] + [jnp.transpose(w, (1, 0, 2)) for w in (w2, w3, w4, w5, w6)]
+    taps[2] = jnp.transpose(w3, (1, 2, 0))
+    return taps + [wo[None, :]]
+
+
+TABLES = [(2, 48, 256), (2, 864, 256), (2, 768, 256), (2, 960, 256), (2, 2, 1504, 256), (2, 864, 256), (512, 128)]
 
 
 def network(edges, n, wh, p, l1, a1, a2, pool, m1, m2, d1, weights, emit):
     t1, t2, t3, t4, t5, t6, th = weights
-    pairs = wh + 8
 
     def rows(j, off, size):
         return pl.ds(pl.multiple_of((j + 4) * n + off, 16), size)
@@ -271,7 +299,7 @@
 
 
 def xz_kernel(edges, v, *refs):
-    weights, (out, vf, pf, hx), scratch = refs[:7], refs[7:11], refs[11:]
+    held, out, weights, (vf, pf, hx), scratch = refs[0], refs[1], refs[2:9], refs[9:12], refs[12:]
     n, wh = 16, 32
     for z in range(16):
         vf[16 * z : 16 * z + 16, :] = v[z].astype(F32)
@@ -281,6 +309,8 @@
     p = scratch[0]
     for x in range(80):
         p[x % 2, 16 * (x // 2) : 16 * (x // 2) + 16, :] = pf[16 * x : 16 * x + 16, 0:16].astype(BF)
+
+    build_tables(held, *weights)
 
     def emit(q, j0, cols, head):
         for k in range(cols):
@@ -342,8 +372,34 @@
                     out[s, z] = rolled[:, 128 * s : 128 * s + 128]
 
 
-SMEM = pl.BlockSpec(memory_space=pltpu.SMEM)
-VMEM = pl.BlockSpec(memory_space=pltpu.VMEM)
+def compute(xz_edges, yz_edges, xz_tissue, yflags, v, before, after, raw):
+    xz, *tables = pl.pallas_call(
+        xz_kernel,
+        out_shape=[jax.ShapeDtypeStruct((16, 16, 64), F32)] + [jax.ShapeDtypeStruct(s, BF) for s in TABLES],
+        in_specs=[SMEM, VMEM, VMEM],
+        out_specs=[VMEM] * 8,
+        scratch_shapes=[pltpu.VMEM((256, 128), F32), pltpu.VMEM((1280, 128), F32), pltpu.VMEM((1024, 128), F32)]
+        + unet_scratch(16, 32),
+        compiler_params=pltpu.CompilerParams(vmem_limit_bytes=24 << 20),
+        cost_estimate=pl.CostEstimate(flops=6_000_000_000, bytes_accessed=6_000_000, transcendentals=0),
+        name="xz",
+    )(xz_edges, v, raw)
+    return pl.pallas_call(
+        yz_kernel,
+        out_shape=jax.ShapeDtypeStruct((16, 2, 16, 64), BF),
+        in_specs=[SMEM, SMEM] + [VMEM] * 12,
+        out_specs=VMEM,
+        scratch_shapes=[
+            pltpu.VMEM((256, 128), F32),
+            pltpu.VMEM((256, 128), F32),
+            pltpu.VMEM((1024, 128), F32),
+            pltpu.VMEM((256, 128), F32),
+        ]
+        + unet_scratch(64, 8),
+        compiler_params=pltpu.CompilerParams(vmem_limit_bytes=24 << 20),
+        cost_estimate=pl.CostEstimate(flops=6_000_000_000, bytes_accessed=6_000_000, transcendentals=0),
+        name="yz",
+    )(yz_edges, xz_tissue, v, before, after, yflags, xz, *tables)
 
 
 def per_device(volume, xz_tissue, yz_tissue, *weights):
@@ -357,7 +413,7 @@
     )(ch[None].astype(jnp.int32), volume)
     moved = lax.all_to_all(packed, "slab", split_axis=0, concat_axis=0, tiled=True)
     v = moved.reshape(16, 16, 128)
-    tables = prepare(*weights)
+    raw = stage(prepare(*weights))
 
     flags = yz_tissue
     for bit in (1, 2, 4, 8):
@@ -373,33 +429,7 @@
     xz_edges = jnp.stack([window == 0, window == 15]).astype(jnp.int32)
     yz_edges = jnp.stack([tile == 0, tile == 15]).astype(jnp.int32)
 
-    xz = pl.pallas_call(
-        xz_kernel,
-        out_shape=jax.ShapeDtypeStruct((16, 16, 64), F32),
-        in_specs=[SMEM] + [VMEM] * 8,
-        out_specs=VMEM,
-        scratch_shapes=[pltpu.VMEM((256, 128), F32), pltpu.VMEM((1280, 128), F32), pltpu.VMEM((1024, 128), F32)]
-        + unet_scratch(16, 32),
-        cost_estimate=pl.CostEstimate(flops=6_000_000_000, bytes_accessed=6_000_000, transcendentals=0),
-        name="xz",
-    )(xz_edges, v, *tables)
-
-    block = pl.pallas_call(
-        yz_kernel,
-        out_shape=jax.ShapeDtypeStruct((16, 2, 16, 64), BF),
-        in_specs=[SMEM, SMEM] + [VMEM] * 12,
-        out_specs=VMEM,
-        scratch_shapes=[
-            pltpu.VMEM((256, 128), F32),
-            pltpu.VMEM((256, 128), F32),
-            pltpu.VMEM((1024, 128), F32),
-            pltpu.VMEM((256, 128), F32),
-        ]
-        + unet_scratch(64, 8),
-        cost_estimate=pl.CostEstimate(flops=6_000_000_000, bytes_accessed=6_000_000, transcendentals=0),
-        name="yz",
-    )(yz_edges, xz_tissue, v, before, after, yflags, xz, *tables)
-
+    block = compute(xz_edges, yz_edges, xz_tissue, yflags, v, before, after, raw)
     back = lax.all_to_all(block, ("slab", "ch"), split_axis=0, concat_axis=0, tiled=True)
     return jnp.transpose(back, (1, 2, 0, 3)).reshape(2, 16, 1024)
 

time: 107 us -> 86 us (0.80)
  local copies, waits for them, and re-layouts: 13.1 us -> 2.2 us
  Pallas kernels: 43.9 us -> 36.8 us
  waiting for transfers between devices: 5.64 us -> 4.03 us
    unnamed x13 -> x6, local copies, waits for them, and re-layouts: 10.3 us -> 1.3 us
    pallas_call x3, Pallas kernels: 42.3 us -> 35.3 us  [the longest x1 16.7 us: compute(): pl.pallas_call(xz_kernel, out_shape=[jax.ShapeDtypeStruct((16, 16, 64), F...]
    ppermute x4, waiting for transfers between devices: 5.63 us -> 4.02 us  [per_device(): other = lax.ppermute(flags, 'tile', [(i, i ^ bit) for i in range(16)])]
    broadcast_in_dim x1 -> x0, local copies, waits for them, and re-layouts: 1.32 us -> none  [prepare(): head = jnp.broadcast_to(wo[:, None], (wo.shape[0], 128))]
  transfers between devices with their start and end apart: 7 -> 7, of which waited for: 3 -> 2; matrix products, arithmetic and copies ran while one was open for 11% -> 1% of each run, Pallas kernels for 23% -> 24%
where the time goes in v1:
time: 86 us; the launch traced here: 85.6 us
  Pallas kernels  36.8 us (43%)
  starting transfers between devices  21.6 us (25%)
  blocking collectives  19.7 us (23%)
  waiting for transfers between devices  4.03 us (5%)
  local copies, waits for them, and re-layouts  2.2 us (3%)
  other arithmetic  1.18 us (1%)
    all_to_all x1, blocking collectives, per_device(): lax.all_to_all(block, ('slab', 'ch'), split_axis=0, concat_axis=0, tiled=...  19.7 us
    pallas_call x1, Pallas kernels, compute(): pl.pallas_call(xz_kernel, out_shape=[jax.ShapeDtypeStruct((16, 16, 64), F...  16.7 us
    pallas_call x1, Pallas kernels, compute(): pl.pallas_call(yz_kernel, out_shape=jax.ShapeDtypeStruct((16, 2, 16, 64),...  16.6 us
    all_to_all x1, starting transfers between devices, per_device(): lax.all_to_all(packed, 'slab', split_axis=0, concat_axis=0, tiled=True)  8.19 us
    ppermute x4, starting transfers between devices, per_device(): other = lax.ppermute(flags, 'tile', [(i, i ^ bit) for i in range(16)])  5.92 us
    ppermute x1, starting transfers between devices, per_device(): after = lax.ppermute(v, 'tile', [(i + 1, i) for i in range(15)])  5.23 us
    ppermute x4, waiting for transfers between devices, per_device(): other = lax.ppermute(flags, 'tile', [(i, i ^ bit) for i in range(16)])  4.02 us
    ppermute x1, starting transfers between devices, per_device(): before = lax.ppermute(v, 'tile', [(i, i + 1) for i in range(15)])  2.29 us
  transfers between devices with their start and end apart: 7, of which 2 were waited for; matrix products, arithmetic and copies ran while one was open for 1% of the time, Pallas kernels for 24%

profile of v1, /device:TPU:9, one launch (start us, length us, event | category | flops | bytes accessed | tf_op | source)
XLA Modules:
  0.0 85.6 jit_solution(8780869159767176867)
XLA Ops:
  0.0 1.2 %collective-permute-start.2 = (s32[8]{0:T(128)}, s32[8]{0:T(128)S(1)}, u32[]{:S(2)}, u32[]{:S(2)}) collective-permute-start(s32[8]{0:T(128)} %param.12), channel_id=1, source_target_pairs={{0,2},{2,0},{4,6},{6,4},{8,10},{10,8},{12,14},{14,12},{16,18},{18,... | collective-permute-start | bytes 104 | tf_op jit(solution)/shard_map/ppermute | solution.py:420
  1.2 1.6 %pack.1 = bf16[8,2,16,128]{3,2,1,0:T(8,128)(2,1)} custom-call(s32[1]{0:T(128)} %bitcast.2.side, bf16[2,16,1024]{2,1,0:T(8,128)(2,1)} %v.1), custom_call_target="tpu_custom_call" | custom-call | tf_op jit(solution)/shard_map/pack/pallas_call | solution.py:407
  2.8 8.2 %all-to-all-start = ((bf16[8,2,16,128]{3,2,1,0:T(8,128)(2,1)}), bf16[8,2,16,128]{3,2,1,0:T(8,128)(2,1)S(1)}, u32[]{:S(2)}, u32[]{:S(2)}) async-start(bf16[8,2,16,128]{3,2,1,0:T(8,128)(2,1)} %pack.1), calls=%async_computation | async-start | bytes 131072 | tf_op jit(solution)/shard_map/all_to_all | solution.py:414
  11.0 0.1 add_convert_fusion.1.edges
  11.0 0.1 add_convert_fusion.edges
  11.1 0.0 collective-permute-done.2
  11.1 0.8 broadcast_select_fusion
  11.9 2.5 %collective-permute-start.3 = (s32[16]{0:T(128)S(1)}, s32[16]{0:T(128)S(1)}, u32[]{:S(2)}, u32[]{:S(2)}) collective-permute-start(s32[16]{0:T(128)S(1)} %broadcast_select_fusion), channel_id=1, source_target_pairs={{0,4},{2,6},{4,0},{6,2},{8,12},{10,14},{12,8},{14,10},{16,20},{18,... | collective-permute-start | bytes 200 | tf_op jit(solution)/shard_map/ppermute | solution.py:420
  14.4 1.5 %collective-permute-done.3 = s32[16]{0:T(128)S(1)} collective-permute-done((s32[16]{0:T(128)S(1)}, s32[16]{0:T(128)S(1)}, u32[]{:S(2)}, u32[]{:S(2)}) %collective-permute-start.3) | collective-permute-done | bytes 96 | tf_op jit(solution)/shard_map/ppermute | solution.py:420
  15.9 0.1 broadcast_select_fusion.1
  15.9 0.2 collective-permute-start.4
  16.1 2.5 %collective-permute-done.4 = s32[32]{0:T(128)S(1)} collective-permute-done((s32[32]{0:T(128)S(1)}, s32[32]{0:T(128)S(1)}, u32[]{:S(2)}, u32[]{:S(2)}) %collective-permute-start.4) | collective-permute-done | bytes 160 | tf_op jit(solution)/shard_map/ppermute | solution.py:420
  18.7 0.1 broadcast_select_fusion.2
  18.8 2.0 %collective-permute-start.5 = (s32[64]{0:T(128)S(1)}, s32[64]{0:T(128)S(1)}, u32[]{:S(2)}, u32[]{:S(2)}) collective-permute-start(s32[64]{0:T(128)S(1)} %broadcast_select_fusion.2), channel_id=1, source_target_pairs={{0,16},{2,18},{4,20},{6,22},{8,24},{10,26},{12,28},{14,30},{16,0},... | collective-permute-start | bytes 776 | tf_op jit(solution)/shard_map/ppermute | solution.py:420
  20.8 2.0 %stage.1.refs_0_ = bf16[10,192,128]{2,1,0:T(8,128)(2,1)} custom-call(bf16[9,32]{1,0:T(8,128)(2,1)} %bitcast.30, bf16[9,32,32]{2,1,0:T(8,128)(2,1)} %bitcast.26, bf16[9,32,64]{2,1,0:T(8,128)(2,1)} %bitcast.27, bf16[9,64,64]{2,1,0:T(8,128)(2,1)} %bitcast.25, bf16[9,32,96]{2,1,0:T(8,128)(2,1)} %bitcast.28, bf16[9,32,32]{2,1,0:T(8,128)(2,1)} %bitcast.29, ...), custom_call_target="tpu_custom_call" | custom-call | tf_op jit(solution)/shard_map/stage/pallas_call | solution.py:133
  22.7 0.0 collective-permute-done.5
  22.8 0.1 broadcast_select_fusion.3
  22.8 0.1 dynamic-slice_bitcast_fusion.yflags
  22.9 0.0 all-to-all-done
  22.9 0.0 copy-start.1
  22.9 2.3 %collective-permute-start = (bf16[16,16,128]{2,1,0:T(8,128)(2,1)S(1)}, bf16[16,16,128]{2,1,0:T(8,128)(2,1)S(1)}, u32[]{:S(2)}, u32[]{:S(2)}) collective-permute-start(bf16[16,16,128]{2,1,0:T(8,128)(2,1)S(1)} %bitcast.20), channel_id=1, source_target_pairs={{0,2},{2,4},{4,6},{6,8},{8,10},{10,12},{12,14},{14,16},{16,18},{18... | collective-permute-start | bytes 196616 | tf_op jit(solution)/shard_map/ppermute | solution.py:425
  25.2 5.2 %collective-permute-start.1 = (bf16[16,16,128]{2,1,0:T(8,128)(2,1)S(1)}, bf16[16,16,128]{2,1,0:T(8,128)(2,1)S(1)}, u32[]{:S(2)}, u32[]{:S(2)}) collective-permute-start(bf16[16,16,128]{2,1,0:T(8,128)(2,1)S(1)} %bitcast.21), channel_id=1, source_target_pairs={{2,0},{4,2},{6,4},{8,6},{10,8},{12,10},{14,12},{16,14},{18,16},{20... | collective-permute-start | bytes 196616 | tf_op jit(solution)/shard_map/ppermute | solution.py:426
  30.4 0.0 copy-start
  30.5 1.0 %copy-done = bf16[10,192,128]{2,1,0:T(8,128)(2,1)S(1)} copy-done((bf16[10,192,128]{2,1,0:T(8,128)(2,1)S(1)}, bf16[10,192,128]{2,1,0:T(8,128)(2,1)}, u32[]{:S(2)}) %copy-start) | copy-done | bytes 491544
  31.5 16.7 %xz.1 = (f32[16,16,64]{2,1,0:T(8,128)S(1)}, bf16[2,48,256]{2,1,0:T(8,128)(2,1)S(1)}, bf16[2,864,256]{2,1,0:T(8,128)(2,1)S(1)}, bf16[2,768,256]{2,1,0:T(8,128)(2,...) custom-call(s32[2]{0:T(128)S(1)} %add_convert_fusion.1.edges, ...), custom_call_target="tpu_custom_call" | custom-call | flops 6000000000 | bytes 6000000 | tf_op jit(solution)/shard_map/xz/pallas_call | solution.py:376
  48.2 0.0 collective-permute-done.before
  48.2 0.0 collective-permute-done.1.after
  48.2 0.0 copy-done.1
  48.2 16.6 %yz.1 = bf16[16,2,16,64]{3,2,1,0:T(8,128)(2,1)S(1)} custom-call(s32[2]{0:T(128)S(1)} %add_convert_fusion.edges, s32[16]{0:T(128)S(1)} %copy-done.1, bf16[16,16,128]{2,1,0:T(8,128)(2,1)S(1)} %bitcast.23, bf16[16,16,128]{2,1,0:T(8,128)(2,1)S(1)} %collective-permute-done.before, bf16[16,16,128]{2,1,0:T(8,128)(2,1)S(1)} %collective-permute-done.1.after, ...), custom_call_target="tpu_custom_call" | custom-call | flops 6000000000 | bytes 6000000 | tf_op jit(solution)/shard_map/yz/pallas_call | solution.py:387
  64.8 0.1 reshape.8
  65.0 19.7 %all_to_all.10 = bf16[16,2,1024]{2,1,0:T(2,128)(2,1)S(1)} all-to-all(bf16[16,2,1024]{2,1,0:T(2,128)(2,1)S(1)} %reshape.8), channel_id=1, replica_groups=mesh['slab'=8,'tile'=16,'ch'=2] {'slab','ch'}, dimensions={0} | all-to-all | bytes 131072 | tf_op jit(solution)/shard_map/all_to_all | solution.py:433
  84.7 0.1 reshape.9
  84.8 0.1 copy.11
  84.9 0.8 reshape.7
Async XLA Ops:
  0.0 11.1 %collective-permute-start.2 = (s32[8]{0:T(128)}, s32[8]{0:T(128)S(1)}, u32[]{:S(2)}, u32[]{:S(2)}) collective-permute-start(s32[8]{0:T(128)} %param.12), channel_id=1, source_target_pairs={{0,2},{2,0},{4,6},{6,4},{8,10},{10,8},{12,14},{14,12},{16,18},{18,... | collective-permute-start | bytes 104 | tf_op jit(solution)/shard_map/ppermute | solution.py:420
  2.8 20.1 %all-to-all-start = ((bf16[8,2,16,128]{3,2,1,0:T(8,128)(2,1)}), bf16[8,2,16,128]{3,2,1,0:T(8,128)(2,1)S(1)}, u32[]{:S(2)}, u32[]{:S(2)}) async-start(bf16[8,2,16,128]{3,2,1,0:T(8,128)(2,1)} %pack.1), calls=%async_computation | async-start | bytes 131072 | tf_op jit(solution)/shard_map/all_to_all | solution.py:414
  11.9 3.9 %collective-permute-start.3 = (s32[16]{0:T(128)S(1)}, s32[16]{0:T(128)S(1)}, u32[]{:S(2)}, u32[]{:S(2)}) collective-permute-start(s32[16]{0:T(128)S(1)} %broadcast_select_fusion), channel_id=1, source_target_pairs={{0,4},{2,6},{4,0},{6,2},{8,12},{10,14},{12,8},{14,10},{16,20},{18,... | collective-permute-start | bytes 200 | tf_op jit(solution)/shard_map/ppermute | solution.py:420
  15.9 2.7 %collective-permute-start.4 = (s32[32]{0:T(128)S(1)}, s32[32]{0:T(128)S(1)}, u32[]{:S(2)}, u32[]{:S(2)}) collective-permute-start(s32[32]{0:T(128)S(1)} %broadcast_select_fusion.1), channel_id=1, source_target_pairs={{0,8},{2,10},{4,12},{6,14},{8,0},{10,2},{12,4},{14,6},{16,24},{18,... | collective-permute-start | bytes 392 | tf_op jit(solution)/shard_map/ppermute | solution.py:420
  18.8 4.0 %collective-permute-start.5 = (s32[64]{0:T(128)S(1)}, s32[64]{0:T(128)S(1)}, u32[]{:S(2)}, u32[]{:S(2)}) collective-permute-start(s32[64]{0:T(128)S(1)} %broadcast_select_fusion.2), channel_id=1, source_target_pairs={{0,16},{2,18},{4,20},{6,22},{8,24},{10,26},{12,28},{14,30},{16,0},... | collective-permute-start | bytes 776 | tf_op jit(solution)/shard_map/ppermute | solution.py:420
  22.9 25.3 %copy-start.1 = (s32[16]{0:T(128)S(1)}, s32[16]{0:T(128)}, u32[]{:S(2)}) copy-start(s32[16]{0:T(128)} %xflags.1) | copy-start | bytes 196
  22.9 25.3 %collective-permute-start = (bf16[16,16,128]{2,1,0:T(8,128)(2,1)S(1)}, bf16[16,16,128]{2,1,0:T(8,128)(2,1)S(1)}, u32[]{:S(2)}, u32[]{:S(2)}) collective-permute-start(bf16[16,16,128]{2,1,0:T(8,128)(2,1)S(1)} %bitcast.20), channel_id=1, source_target_pairs={{0,2},{2,4},{4,6},{6,8},{8,10},{10,12},{12,14},{14,16},{16,18},{18... | collective-permute-start | bytes 196616 | tf_op jit(solution)/shard_map/ppermute | solution.py:425
  25.2 23.0 %collective-permute-start.1 = (bf16[16,16,128]{2,1,0:T(8,128)(2,1)S(1)}, bf16[16,16,128]{2,1,0:T(8,128)(2,1)S(1)}, u32[]{:S(2)}, u32[]{:S(2)}) collective-permute-start(bf16[16,16,128]{2,1,0:T(8,128)(2,1)S(1)} %bitcast.21), channel_id=1, source_target_pairs={{2,0},{4,2},{6,4},{8,6},{10,8},{12,10},{14,12},{16,14},{18,16},{20... | collective-permute-start | bytes 196616 | tf_op jit(solution)/shard_map/ppermute | solution.py:426
  30.4 1.0 %copy-start = (bf16[10,192,128]{2,1,0:T(8,128)(2,1)S(1)}, bf16[10,192,128]{2,1,0:T(8,128)(2,1)}, u32[]{:S(2)}) copy-start(bf16[10,192,128]{2,1,0:T(8,128)(2,1)} %stage.1.refs_0_) | copy-start | bytes 1474564

commit v2 on v1

--- a/solution.py
+++ b/solution.py
@@ -5,7 +5,6 @@
 from jax.experimental.pallas import tpu as pltpu
 from jax.sharding import PartitionSpec as P
 
-
 BF = jnp.bfloat16
 F32 = jnp.float32
 SMEM = pl.BlockSpec(memory_space=pltpu.SMEM)
@@ -33,32 +32,41 @@
     return jnp.concatenate([tap] * cells, axis=0)
 
 
-def build_tables(held, t1, t2, t3, t4, t5, t6, th):
-    def part(first, last):
-        return lambda t, lo, hi: held[t, first:last, lo:hi]
-
-    w2, w3, w4, w5, w6 = part(0, 32), part(32, 64), part(64, 128), part(128, 160), part(160, 192)
-
-    def fine(src, dst, lo, hi, base):
-        row, lane = iota((256, 256), 0) // 32, iota((256, 256), 1) // 32
-        g = [spread(src(t, lo, hi), 8, True) for t in range(9)]
-        edge = iota((32, 256), 1) // 32
-        for s in range(3):
-            tile = jnp.zeros((256, 256), F32)
-            for r in range(3):
-                tile = jnp.where(row == lane + (r - 1), stack_rows(g[3 * r + s], 8), tile)
-            tile = tile.astype(BF)
-            below = jnp.where(edge == 7, g[6 + s], 0.0).astype(BF)
-            above = jnp.where(edge == 0, g[s], 0.0).astype(BF)
-            for d in dst:
-                d[0, 256 * s : 256 * s + 256, :] = tile
-                d[1, 256 * s : 256 * s + 256, :] = tile
-                d[0, base + 32 * s : base + 32 * s + 32, :] = below
-                d[1, base + 32 * s : base + 32 * s + 32, :] = above
-
-    fine(w2, [t2], 0, 32, 768)
-    fine(w6, [t6], 0, 32, 768)
-    fine(w5, [t5.at[0], t5.at[1]], 64, 96, 1280)
+def taps_of(held, first, last):
+    return lambda t, lo, hi: held[t, first:last, lo:hi]
+
+
+def fine(src, lo, hi, base, own, edges, merged):
+    row, lane = iota((256, 256), 0) // 32, iota((256, 256), 1) // 32
+    g = [spread(src(t, lo, hi), 8, True) for t in range(9)]
+    edge = iota((32, 256), 1) // 32
+    for s in range(3):
+        tile = jnp.zeros((256, 256), F32)
+        for r in range(3):
+            tile = jnp.where(row == lane + (r - 1), stack_rows(g[3 * r + s], 8), tile)
+        tile = tile.astype(BF)
+        for d in own:
+            d[256 * s : 256 * s + 256, :] = tile
+        for h, near, taps in ((0, 7, g[6 + s]), (1, 0, g[s])):
+            for d in edges:
+                d[h, base + 32 * s : base + 32 * s + 32, :] = jnp.where(edge == near, taps, 0.0).astype(BF)
+    for d in merged:
+        for h in range(2):
+            for k in range(4):
+                tile = jnp.zeros((32, 256), F32)
+                for q in range(2):
+                    s = k - q
+                    if 0 <= s < 3:
+                        near = (7, 3)[q] if h == 0 else (0, 4)[q]
+                        tile = jnp.where(edge == near, g[6 + s] if h == 0 else g[s], tile)
+                d[128 * h + 32 * k : 128 * h + 32 * k + 32, :] = tile.astype(BF)
+
+
+def build_tables(held, t1, t2, t3, t4, t6):
+    w2, w3, w4, w6 = taps_of(held, 0, 32), taps_of(held, 32, 64), taps_of(held, 64, 128), taps_of(held, 160, 192)
+
+    fine(w2, 0, 32, 0, [t2.at[0:768]], [], [t2.at[768:1024]])
+    fine(w6, 0, 32, 0, [t6.at[0:768]], [], [t6.at[768:1024]])
 
     row, lane = iota((16, 256), 0), iota((16, 256), 1) // 32
     first = spread(held[9, 0:16, 0:32], 8, False)
@@ -71,13 +79,14 @@
             t1[h, 16 * s : 16 * s + 16, :] = tile.astype(BF)
 
     row, lane = iota((256, 256), 0) // 32, iota((256, 256), 1) // 64
+    row = row // 2 + 4 * (row % 2)
     g = [spread(w3(t, 0, 64), 4, False) for t in range(9)]
     for s in range(3):
         for h in range(2):
             tile = jnp.zeros((256, 256), F32)
             for r in range(3):
                 tile = jnp.where(row == lane + 4 * h + (r - 1), stack_rows(g[3 * r + s], 8), tile)
-            t3[h, 256 * s : 256 * s + 256, :] = tile.astype(BF)
+            t3[256 * s : 256 * s + 256, 256 * h : 256 * h + 256] = tile.astype(BF)
 
     row, lane = iota((256, 256), 0) // 64, iota((256, 256), 1) // 64
     edge = iota((64, 256), 1) // 64
@@ -91,6 +100,11 @@
             t4[h, 256 * s : 256 * s + 256, :] = tile
         t4[0, 768 + 64 * s : 832 + 64 * s, :] = jnp.where(edge == 3, g[6 + s], 0.0).astype(BF)
         t4[1, 768 + 64 * s : 832 + 64 * s, :] = jnp.where(edge == 0, g[s], 0.0).astype(BF)
+
+
+def build_join(held, t5, th):
+    w5 = taps_of(held, 128, 160)
+    fine(w5, 64, 96, 1280, [t5.at[q, h] for q in range(2) for h in range(2)], [t5.at[0], t5.at[1]], [])
 
     row, lane = iota((256, 256), 0) // 64, iota((256, 256), 1) // 32
     edge = iota((64, 256), 1) // 32
@@ -145,7 +159,8 @@
     return taps + [wo[None, :]]
 
 
-TABLES = [(2, 48, 256), (2, 864, 256), (2, 768, 256), (2, 960, 256), (2, 2, 1504, 256), (2, 864, 256), (512, 128)]
+TABLES = [(2, 48, 256), (1024, 256), (768, 512), (2, 960, 256), (1024, 256)]
+JOIN = [(2, 2, 1504, 256), (512, 128)]
 
 
 def network(edges, n, wh, p, l1, a1, a2, pool, m1, m2, d1, weights, emit):
@@ -187,101 +202,99 @@
         for s, (qs, dj) in enumerate(near(q)):
             l1[q, rows(j0, 0, size), 16 * s : 16 * s + 16] = p[qs, rows(j0 + dj, 0, size), :]
 
+    c2, c6 = (wh + 6) // 2, wh // 2
+
     def relu(v):
         return jnp.maximum(v, 0.0).astype(BF)
 
     c1 = {15: 5, 39: 13}[wh + 7]
-    for q in range(2):
-        j0 = -3 if q == 0 else -4
-
-        def body(dj, off, size, q=q, j0=j0):
-            r = rows(j0, off, size)
+
+    def first(dj, off, size):
+        for q in range(2):
+            r = rows(-3 - q, off, size)
             x = l1[q, r, 0:48]
             for h in range(2):
                 a1[q, h, r, :] = relu(dot(x, t1[h]))
 
-        loop(wh + 7, c1, body)
+    loop(wh + 7, c1, first)
     clear(a1, four, 4)
 
-    def fine_inputs(src, q, h, j0, off, size):
-        other = slice(0, 32) if h == 0 else slice(224, 256)
-        own = [src[qs, h, rows(j0 + dj, off, size), :] for qs, dj in near(q)]
-        edge = [src[qs, 1 - h, rows(j0 + dj, off, size), other] for qs, dj in near(q)]
-        return own, edge
-
-    c2 = (wh + 6) // 2
-    for q, h in four:
-
-        def body(dj, off, size, q=q, h=h):
-            own, edge = fine_inputs(a1, q, h, -3, off, size)
-            a2[q, h, rows(-3, off, size), :] = relu(dot(jnp.concatenate(own + edge, axis=1), t2[h]))
-
-        loop(wh + 6, c2, body)
+    def fine_conv(src, table, j0, off, size):
+        ends = []
+        for half, lanes in ((1, slice(0, 32)), (0, slice(224, 256))):
+            ends += [src[q, half, rows(j0 + dj, off, size), lanes] for q, dj in ((1, -1), (0, 0), (1, 0), (0, 1))]
+        extra = dot(jnp.concatenate(ends, axis=1), table[768:1024, :])
+        low, high = extra[:, 0:128], extra[:, 128:256]
+        lane = iota((size, 128), 1)
+        outs = {}
+        for q, h in four:
+            own = [src[qs, h, rows(j0 + dj, off, size), :] for qs, dj in near(q)]
+            acc = dot(jnp.concatenate(own, axis=1), table[0:768, :])
+            left, right = acc[:, 0:128], acc[:, 128:256]
+            if h == 0:
+                right = right + jnp.where(lane >= 96, high if q == 0 else low, 0.0)
+            else:
+                left = left + jnp.where(lane < 32, low if q == 0 else high, 0.0)
+            outs[q, h] = relu(left), relu(right)
+        return outs
+
+    def second(dj, off, size):
+        outs = fine_conv(a1, t2, -3, off, size)
+        r = rows(-3, off, size)
+        for q, h in four:
+            for i in range(2):
+                a2[q, h, r, 128 * i : 128 * i + 128] = outs[q, h][i]
+        even = iota((size, 128), 1) % 64 < 32
+        for i in range(2):
+            sums = [outs[0, h][i].astype(F32) + outs[1, h][i].astype(F32) for h in range(2)]
+            sums = [sums[0] + pltpu.roll(sums[0], 96, 1), sums[1] + pltpu.roll(sums[1], 32, 1)]
+            pool[r, 128 * i : 128 * i + 128] = (0.25 * jnp.where(even, sums[0], sums[1])).astype(BF)
+
+    loop(wh + 6, c2, second)
     clear(a2, four, 3)
-
-    def pick_pool():
-        shape = (1024, 256)
-        row, lane = iota(shape, 0), iota(shape, 1)
-        cell = 4 * (row // 512) + ((row // 32) % 8) // 2
-        return jnp.where((cell == lane // 32) & (row % 32 == lane % 32), 0.25, 0.0).astype(BF)
-
-    pm = pick_pool()
-
-    def body(dj, off, size):
-        r = rows(-3, off, size)
-        x = jnp.concatenate([a2[0, 0, r, :], a2[1, 0, r, :], a2[0, 1, r, :], a2[1, 1, r, :]], axis=1)
-        pool[r, :] = dot(x, pm).astype(BF)
-
-    loop(wh + 6, c2, body)
-
-    c3 = (wh + 4) // 2
-
-    def body(dj, off, size):
+    clear(pool, [()], 3)
+
+    def third(dj, off, size):
         x = jnp.concatenate([pool[rows(-2 + k, off, size), :] for k in (-1, 0, 1)], axis=1)
-        for h in range(2):
-            m1[h, rows(-2, off, size), :] = relu(dot(x, t3[h]))
-
-    loop(wh + 4, c3, body)
+        y = relu(dot(x, t3[...]))
+        for h in range(2):
+            m1[h, rows(-2, off, size), :] = y[:, 256 * h : 256 * h + 256]
+
+    loop(wh + 4, (wh + 4) // 2, third)
     clear(m1, both, 2)
 
-    c4 = (wh + 2) // 2
-    for h in range(2):
-
-        def body(dj, off, size, h=h):
+    def fourth(dj, off, size):
+        for h in range(2):
             other = slice(0, 64) if h == 0 else slice(192, 256)
             own = [m1[h, rows(-1 + k, off, size), :] for k in (-1, 0, 1)]
             edge = [m1[1 - h, rows(-1 + k, off, size), other] for k in (-1, 0, 1)]
             m2[h, rows(-1, off, size), :] = relu(dot(jnp.concatenate(own + edge, axis=1), t4[h]))
 
-        loop(wh + 2, c4, body)
+    loop(wh + 2, (wh + 2) // 2, fourth)
     clear(m2, both, 1)
 
-    c5 = {9: 3, 33: 11}[wh + 1]
-    for q, h in four:
-        j0 = 0 if q == 0 else -1
-
-        def body(dj, off, size, q=q, h=h, j0=j0):
-            own, edge = fine_inputs(a2, q, h, j0, off, size)
+    def fifth(dj, off, size):
+        for q, h in four:
+            j0 = -q
+            other = slice(0, 32) if h == 0 else slice(224, 256)
+            own = [a2[qs, h, rows(j0 + k, off, size), :] for qs, k in near(q)]
+            edge = [a2[qs, 1 - h, rows(j0 + k, off, size), other] for qs, k in near(q)]
             other = slice(0, 64) if h == 0 else slice(192, 256)
             cells = (-1, 0) if q == 0 else (0, 1)
             own += [m2[h, rows(j0 + k, off, size), :] for k in cells]
             edge += [m2[1 - h, rows(j0 + k, off, size), other] for k in cells]
             d1[q, h, rows(j0, off, size), :] = relu(dot(jnp.concatenate(own + edge, axis=1), t5[q, h]))
 
-        loop(wh + 1, c5, body)
+    loop(wh + 1, {9: 3, 33: 11}[wh + 1], fifth)
     clear(d1, four, 1)
 
-    c6 = wh // 2
-    for q in range(2):
-
-        def body(dj, off, size, q=q):
-            parts = []
-            for h in range(2):
-                own, edge = fine_inputs(d1, q, h, 0, off, size)
-                parts.append(relu(dot(jnp.concatenate(own + edge, axis=1), t6[h])))
-            emit(q, dj, c6, dot(jnp.concatenate(parts, axis=1), th[...]))
-
-        loop(wh, c6, body)
+    def sixth(dj, off, size):
+        outs = fine_conv(d1, t6, 0, off, size)
+        for q in range(2):
+            x = jnp.concatenate(outs[q, 0] + outs[q, 1], axis=1)
+            emit(q, dj, c6, dot(x, th[...]))
+
+    loop(wh, c6, sixth)
 
 
 def unet_scratch(n, wh):
@@ -299,7 +312,8 @@
 
 
 def xz_kernel(edges, v, *refs):
-    held, out, weights, (vf, pf, hx), scratch = refs[0], refs[1], refs[2:9], refs[9:12], refs[12:]
+    held, out, tables, (vf, pf, hx), join, scratch = refs[0], refs[1], refs[2:7], refs[7:10], refs[10:12], refs[12:]
+    weights = (*tables[:4], join[0], tables[4], join[1])
     n, wh = 16, 32
     for z in range(16):
         vf[16 * z : 16 * z + 16, :] = v[z].astype(F32)
@@ -310,7 +324,8 @@
     for x in range(80):
         p[x % 2, 16 * (x // 2) : 16 * (x // 2) + 16, :] = pf[16 * x : 16 * x + 16, 0:16].astype(BF)
 
-    build_tables(held, *weights)
+    build_tables(held, *tables)
+    build_join(held, *join)
 
     def emit(q, j0, cols, head):
         for k in range(cols):
@@ -322,23 +337,50 @@
         out[y] = jnp.transpose(hx[pl.ds(y, 64, stride=16), :])[0:16, :]
 
 
-def yz_kernel(edges, xflags, v, before, after, yflags, xz, *refs):
-    weights, (out, vf, hf, hy, rf), scratch = refs[:7], refs[7:12], refs[12:]
+def spread_kernel(place, v, row, out):
+    t = place[0]
+    lane = iota((16, 128), 1)
+    pairs = []
+    for z in range(8):
+        low = pltpu.roll(v[z].astype(F32), 128 - HALO, 1)
+        high = pltpu.roll(v[z + 8].astype(F32), 64 - HALO, 1)
+        pairs.append(jnp.where(lane < 64, low, high))
+    last = [jnp.concatenate([pairs[2 * k][8:], pairs[2 * k + 1][8:]], axis=0).astype(BF) for k in range(4)]
+    first = [jnp.concatenate([pairs[2 * k][:8], pairs[2 * k + 1][:8]], axis=0).astype(BF) for k in range(4)]
+    for p in range(16):
+        for rows, cond in ((last, t < p), (first, t >= p)):
+
+            @pl.when(cond)
+            def _(p=p, rows=rows):
+                for k in range(4):
+                    out[p, k] = rows[k]
+
+        out[p, 4] = row[...]
+
+
+def yz_kernel(edges, xflags, v, shared, xz, *refs):
+    tables, held, (out, vf, hf, hy, rf), join, scratch = refs[:5], refs[5], refs[6:11], refs[11:13], refs[13:]
+    weights = (*tables[:4], join[0], tables[4], join[1])
+    build_join(held, *join)
     n, wh = 64, 8
     p = scratch[0]
+    tile, octet = edges[2], 8 * edges[3]
     for z in range(16):
         vf[16 * z : 16 * z + 16, :] = v[z].astype(F32)
-        hf[16 * z : 16 * z + 8, :] = before[z, 8:16, :].astype(F32)
-        hf[16 * z + 8 : 16 * z + 16, :] = after[z, 0:8, :].astype(F32)
+    for side, source in ((0, jnp.maximum(tile - 1, 0)), (1, jnp.minimum(tile + 1, 15))):
+        for k in range(4):
+            both = shared[source, k].astype(F32)
+            for i in range(2):
+                at = 16 * (2 * k + i) + 8 * side
+                hf[at : at + 8, :] = both[8 * i : 8 * i + 8, :]
     for k in range(32):
-        if k < 8:
-            plane = hf[pl.ds(k, 16, stride=16), :]
-        elif k < 24:
-            plane = vf[pl.ds(k - 8, 16, stride=16), :]
+        at = slice(n * (k // 2), n * (k // 2) + n)
+        if 8 <= k < 24:
+            turned = jnp.transpose(vf[pl.ds(k - 8, 16, stride=16), :])
+            p[k % 2, at, :] = turned[HALO : HALO + n, :].astype(BF)
         else:
-            plane = hf[pl.ds(k - 16, 16, stride=16), :]
-        turned = jnp.transpose(plane)
-        p[k % 2, n * (k // 2) : n * (k // 2) + n, :] = turned[HALO : HALO + n, :].astype(BF)
+            turned = jnp.transpose(hf[pl.ds(k if k < 8 else k - 16, 8, stride=16), :])
+            p[k % 2, at, :] = jnp.concatenate([turned[0:n, :], turned[n:, :]], axis=1).astype(BF)
 
     def emit(q, j0, cols, head):
         for k in range(cols):
@@ -347,7 +389,7 @@
 
     network(edges, n, wh, *scratch, weights, emit)
 
-    yes = yflags[...] > 0
+    yes = sum(shared[octet + i, 4].astype(F32) for i in range(8))[0:1, 0:64] > 0.5
     for y in range(16):
         plane = pltpu.roll(vf[pl.ds(y, 16, stride=16), :], 128 - HALO, 1)[:, 0:64]
         yz = jnp.transpose(hy[64 * y : 64 * y + 64, :])[0:16, :]
@@ -372,13 +414,14 @@
                     out[s, z] = rolled[:, 128 * s : 128 * s + 128]
 
 
-def compute(xz_edges, yz_edges, xz_tissue, yflags, v, before, after, raw):
+def compute(xz_edges, yz_edges, xz_tissue, v, shared, raw):
     xz, *tables = pl.pallas_call(
         xz_kernel,
         out_shape=[jax.ShapeDtypeStruct((16, 16, 64), F32)] + [jax.ShapeDtypeStruct(s, BF) for s in TABLES],
         in_specs=[SMEM, VMEM, VMEM],
-        out_specs=[VMEM] * 8,
+        out_specs=[VMEM] * 6,
         scratch_shapes=[pltpu.VMEM((256, 128), F32), pltpu.VMEM((1280, 128), F32), pltpu.VMEM((1024, 128), F32)]
+        + [pltpu.VMEM(s, BF) for s in JOIN]
         + unet_scratch(16, 32),
         compiler_params=pltpu.CompilerParams(vmem_limit_bytes=24 << 20),
         cost_estimate=pl.CostEstimate(flops=6_000_000_000, bytes_accessed=6_000_000, transcendentals=0),
@@ -387,19 +430,20 @@
     return pl.pallas_call(
         yz_kernel,
         out_shape=jax.ShapeDtypeStruct((16, 2, 16, 64), BF),
-        in_specs=[SMEM, SMEM] + [VMEM] * 12,
+        in_specs=[SMEM, SMEM] + [VMEM] * 9,
         out_specs=VMEM,
         scratch_shapes=[
             pltpu.VMEM((256, 128), F32),
-            pltpu.VMEM((256, 128), F32),
+            pltpu.VMEM((128, 128), F32),
             pltpu.VMEM((1024, 128), F32),
             pltpu.VMEM((256, 128), F32),
         ]
+        + [pltpu.VMEM(s, BF) for s in JOIN]
         + unet_scratch(64, 8),
         compiler_params=pltpu.CompilerParams(vmem_limit_bytes=24 << 20),
         cost_estimate=pl.CostEstimate(flops=6_000_000_000, bytes_accessed=6_000_000, transcendentals=0),
         name="yz",
-    )(yz_edges, xz_tissue, v, before, after, yflags, xz, *tables)
+    )(yz_edges, xz_tissue, v, shared, xz, *tables, raw)
 
 
 def per_device(volume, xz_tissue, yz_tissue, *weights):
@@ -415,21 +459,23 @@
     v = moved.reshape(16, 16, 128)
     raw = stage(prepare(*weights))
 
-    flags = yz_tissue
-    for bit in (1, 2, 4, 8):
-        other = lax.ppermute(flags, "tile", [(i, i ^ bit) for i in range(16)])
-        high = (tile & bit) > 0
-        flags = jnp.where(high, jnp.concatenate([other, flags]), jnp.concatenate([flags, other]))
-    yflags = lax.dynamic_slice_in_dim(flags, 64 * ch, 64, 0)[None, :]
-
-    before = lax.ppermute(v, "tile", [(i, i + 1) for i in range(15)])
-    after = lax.ppermute(v, "tile", [(i + 1, i) for i in range(15)])
+    mine = (jnp.arange(128) // 8 == tile % 8)[None, :]
+    row = jnp.where(mine, jnp.tile(yz_tissue, 16)[None, :], 0).astype(BF)
+    shared = pl.pallas_call(
+        spread_kernel,
+        out_shape=jax.ShapeDtypeStruct((16, 5, 16, 128), BF),
+        in_specs=[SMEM, VMEM, VMEM],
+        out_specs=VMEM,
+        compiler_params=pltpu.CompilerParams(vmem_limit_bytes=8 << 20),
+        name="spread",
+    )(tile[None].astype(jnp.int32), v, jnp.broadcast_to(row, (16, 128)))
+    shared = lax.all_to_all(shared, "tile", split_axis=0, concat_axis=0, tiled=True)
 
     window = 2 * slab + ch
     xz_edges = jnp.stack([window == 0, window == 15]).astype(jnp.int32)
-    yz_edges = jnp.stack([tile == 0, tile == 15]).astype(jnp.int32)
-
-    block = compute(xz_edges, yz_edges, xz_tissue, yflags, v, before, after, raw)
+    yz_edges = jnp.stack([tile == 0, tile == 15, tile, ch]).astype(jnp.int32)
+
+    block = compute(xz_edges, yz_edges, xz_tissue, v, shared, raw)
     back = lax.all_to_all(block, ("slab", "ch"), split_axis=0, concat_axis=0, tiled=True)
     return jnp.transpose(back, (1, 2, 0, 3)).reshape(2, 16, 1024)
 

time: 86 us -> 66.6 us (0.77)
  Pallas kernels: 36.8 us -> 28.8 us
  blocking collectives: 19.7 us -> 12.9 us
  starting transfers between devices: 21.6 us -> 15 us
  local copies, waits for them, and re-layouts: 2.2 us -> 4.35 us
  other arithmetic: 1.18 us -> 0.16 us
    ppermute x6 -> x0, starting transfers between devices: 13.4 us -> none  [the longest x4 5.92 us: per_device(): other = lax.ppermute(flags, 'tile', [(i, i ^ bit) for i in range(16)])]
    all_to_all x0 -> x1, starting transfers between devices: none -> 6.83 us  [per_device(): lax.all_to_all(shared, 'tile', split_axis=0, concat_axis=0, tiled=True)]
    all_to_all x1, blocking collectives: 19.7 us -> 12.9 us  [per_device(): lax.all_to_all(block, ('slab', 'ch'), split_axis=0, concat_axis=0, tiled=...]
    pallas_call x1, Pallas kernels: 16.7 us -> 11.9 us  [compute(): pl.pallas_call(xz_kernel, out_shape=[jax.ShapeDtypeStruct((16, 16, 64), F...]
    all_to_all x1, waiting for transfers between devices: 0.01 us -> 4.37 us  [per_device(): lax.all_to_all(packed, 'slab', split_axis=0, concat_axis=0, tiled=True)]
    pallas_call x1, Pallas kernels: 16.6 us -> 12.5 us  [compute(): pl.pallas_call(yz_kernel, out_shape=jax.ShapeDtypeStruct((16, 2, 16, 64),...]
    ppermute x6 -> x0, waiting for transfers between devices: 4.03 us -> none  [the longest x4 4.02 us: per_device(): other = lax.ppermute(flags, 'tile', [(i, i ^ bit) for i in range(16)])]
    unnamed x6 -> x12, local copies, waits for them, and re-layouts: 1.3 us -> 3.43 us
  transfers between devices with their start and end apart: 7 -> 2, of which waited for: 2 -> 1; matrix products, arithmetic and copies ran while one was open for 1% -> 0% of each run, Pallas kernels for 24% -> 21%
where the time goes in v2:
time: 66.6 us; the launch traced here: 65.6 us
  Pallas kernels  28.8 us (43%)
  starting transfers between devices  15 us (23%)
  blocking collectives  12.9 us (19%)
  waiting for transfers between devices  4.37 us (7%)
  local copies, waits for them, and re-layouts  4.35 us (7%)
    all_to_all x1, blocking collectives, per_device(): lax.all_to_all(block, ('slab', 'ch'), split_axis=0, concat_axis=0, tiled=...  12.9 us
    pallas_call x1, Pallas kernels, compute(): pl.pallas_call(yz_kernel, out_shape=jax.ShapeDtypeStruct((16, 2, 16, 64),...  12.5 us
    pallas_call x1, Pallas kernels, compute(): pl.pallas_call(xz_kernel, out_shape=[jax.ShapeDtypeStruct((16, 16, 64), F...  11.9 us
    all_to_all x1, starting transfers between devices, per_device(): lax.all_to_all(packed, 'slab', split_axis=0, concat_axis=0, tiled=True)  8.19 us
    all_to_all x1, starting transfers between devices, per_device(): lax.all_to_all(shared, 'tile', split_axis=0, concat_axis=0, tiled=True)  6.83 us
    all_to_all x1, waiting for transfers between devices, per_device(): lax.all_to_all(packed, 'slab', split_axis=0, concat_axis=0, tiled=True)  4.37 us
    unnamed x12, local copies, waits for them, and re-layouts  3.43 us
    pallas_call x1, Pallas kernels, stage(): pl.pallas_call(stage_kernel, out_shape=jax.ShapeDtypeStruct((10, 192, 128...  1.94 us
  transfers between devices with their start and end apart: 2, of which 1 were waited for; matrix products, arithmetic and copies ran while one was open for 0% of the time, Pallas kernels for 21%

profile of v2, /device:TPU:9, one launch (start us, length us, event | category | flops | bytes accessed | tf_op | source)
XLA Modules:
  0.0 65.6 jit_solution(9443510616389504086)
XLA Ops:
  0.0 1.6 %pack.1 = bf16[8,2,16,128]{3,2,1,0:T(8,128)(2,1)} custom-call(s32[1]{0:T(128)} %bitcast.3.side, bf16[2,16,1024]{2,1,0:T(8,128)(2,1)} %v.1), custom_call_target="tpu_custom_call" | custom-call | tf_op jit(solution)/shard_map/pack/pallas_call | solution.py:451
  1.6 8.2 %all-to-all-start = ((bf16[8,2,16,128]{3,2,1,0:T(8,128)(2,1)}), bf16[8,2,16,128]{3,2,1,0:T(8,128)(2,1)S(1)}, u32[]{:S(2)}, u32[]{:S(2)}) async-start(bf16[8,2,16,128]{3,2,1,0:T(8,128)(2,1)} %pack.1), calls=%async_computation | async-start | bytes 131072 | tf_op jit(solution)/shard_map/all_to_all | solution.py:458
  9.7 0.0 copy-start.4
  9.7 0.7 copy-done.4
  10.4 0.1 broadcast_in_dim_tile.3
  10.5 0.1 add_convert_fusion.edges
  10.6 1.9 %stage.1.refs_0_.refs_5_ = bf16[10,192,128]{2,1,0:T(8,128)(2,1)} custom-call(bf16[9,32]{1,0:T(8,128)(2,1)} %bitcast.28, bf16[9,32,32]{2,1,0:T(8,128)(2,1)} %bitcast.24, bf16[9,32,64]{2,1,0:T(8,128)(2,1)} %bitcast.25, bf16[9,64,64]{2,1,0:T(8,128)(2,1)} %bitcast.23, bf16[9,32,96]{2,1,0:T(8,128)(2,1)} %bitcast.26, bf16[9,32,32]{2,1,0:T(8,128)(2,1)} %bitcast.27, ...), custom_call_target="tpu_custom_call" | custom-call | tf_op jit(solution)/shard_map/stage/pallas_call | solution.py:147
  12.5 0.1 pad_add_fusion.edges
  12.6 4.4 %all-to-all-done = bf16[8,2,16,128]{3,2,1,0:T(8,128)(2,1)S(1)} async-done(((bf16[8,2,16,128]{3,2,1,0:T(8,128)(2,1)}), bf16[8,2,16,128]{3,2,1,0:T(8,128)(2,1)S(1)}, u32[]{:S(2)}, u32[]{:S(2)}) %all-to-all-start) | async-done | bytes 65568 | tf_op jit(solution)/shard_map/all_to_all | solution.py:458
  17.0 0.0 copy-start
  17.0 0.9 %spread.1 = bf16[16,5,16,128]{3,2,1,0:T(8,128)(2,1)} custom-call(s32[1]{0:T(128)} %bitcast.2.place, bf16[16,16,128]{2,1,0:T(8,128)(2,1)S(1)} %bitcast.19, bf16[16,128]{1,0:T(8,128)(2,1)S(1)} %broadcast_in_dim.6.row), custom_call_target="tpu_custom_call" | custom-call | tf_op jit(solution)/shard_map/spread/pallas_call | solution.py:464
  17.9 6.8 %all-to-all-start.1 = ((bf16[16,5,16,128]{3,2,1,0:T(8,128)(2,1)}), bf16[16,5,16,128]{3,2,1,0:T(8,128)(2,1)S(1)}, u32[]{:S(2)}, u32[]{:S(2)}) async-start(bf16[16,5,16,128]{3,2,1,0:T(8,128)(2,1)} %spread.1), calls=%async_computation.1 | async-start | bytes 655360 | tf_op jit(solution)/shard_map/all_to_all | solution.py:472
  24.7 0.0 copy-done
  24.8 11.9 %xz.1 = (f32[16,16,64]{2,1,0:T(8,128)S(1)}, bf16[2,48,256]{2,1,0:T(8,128)(2,1)S(1)}, bf16[1024,256]{1,0:T(8,128)(2,1)S(1)}, bf16[768,512]{1,0:T(8,128)(2,1)S(1)}...) custom-call(s32[2]{0:T(128)S(1)} %add_convert_fusion.edges, bf16[16,16,128]{2,1,0:T(8,128)(2,1)S(1)} %bitcast.20, ...), custom_call_target="tpu_custom_call" | custom-call | flops 6000000000 | bytes 6000000 | tf_op jit(solution)/shard_map/xz/pallas_call | solution.py:418
  36.7 0.0 copy-start.2
  36.7 0.8 %copy-done.2 = bf16[1024,256]{1,0:T(8,128)(2,1)} copy-done((bf16[1024,256]{1,0:T(8,128)(2,1)}, bf16[1024,256]{1,0:T(8,128)(2,1)S(1)}, u32[]{:S(2)}) %copy-start.2) | copy-done | bytes 524312
  37.5 0.0 all-to-all-done.1.shared
  37.5 0.0 copy-start.1
  37.5 0.7 copy-done.1
  38.1 0.0 copy-start.3
  38.1 1.0 %copy-done.3 = bf16[1024,256]{1,0:T(8,128)(2,1)S(1)} copy-done((bf16[1024,256]{1,0:T(8,128)(2,1)S(1)}, bf16[1024,256]{1,0:T(8,128)(2,1)}, u32[]{:S(2)}) %copy-start.3) | copy-done | bytes 524312
  39.2 12.5 %yz.1 = bf16[16,2,16,64]{3,2,1,0:T(8,128)(2,1)S(1)} custom-call(s32[4]{0:T(128)S(1)} %pad_add_fusion.edges, s32[16]{0:T(128)S(1)} %copy-done.1, bf16[16,16,128]{2,1,0:T(8,128)(2,1)S(1)} %bitcast.21, bf16[16,5,16,128]{3,2,1,0:T(8,128)(2,1)S(1)} %all-to-all-done.1.shared, f32[16,16,64]{2,1,0:T(8,128)S(1)} %get-tuple-element.11.xz, ...), custom_call_target="tpu_custom_call" | custom-call | flops 6000000000 | bytes 6000000 | tf_op jit(solution)/shard_map/yz/pallas_call | solution.py:430
  51.6 0.1 reshape.34
  51.8 12.9 %all_to_all.15 = bf16[16,2,1024]{2,1,0:T(2,128)(2,1)S(1)} all-to-all(bf16[16,2,1024]{2,1,0:T(2,128)(2,1)S(1)} %reshape.34), channel_id=1, replica_groups=mesh['slab'=8,'tile'=16,'ch'=2] {'slab','ch'}, dimensions={0} | all-to-all | bytes 131072 | tf_op jit(solution)/shard_map/all_to_all | solution.py:479
  64.7 0.1 reshape.35
  64.8 0.1 copy.11
  64.9 0.8 %reshape.31 = bf16[2,16,1024]{2,1,0:T(8,128)(2,1)} reshape(bf16[2,16,16,64]{3,2,1,0:T(8,128)(2,1)S(1)} %copy.11) | data formatting | bytes 131072 | tf_op jit(solution)/shard_map/reshape | solution.py:480
  (3 shorter events, 0.0 us)
Async XLA Ops:
  1.6 15.4 %all-to-all-start = ((bf16[8,2,16,128]{3,2,1,0:T(8,128)(2,1)}), bf16[8,2,16,128]{3,2,1,0:T(8,128)(2,1)S(1)}, u32[]{:S(2)}, u32[]{:S(2)}) async-start(bf16[8,2,16,128]{3,2,1,0:T(8,128)(2,1)} %pack.1), calls=%async_computation | async-start | bytes 131072 | tf_op jit(solution)/shard_map/all_to_all | solution.py:458
  9.7 0.7 copy-start.4
  17.0 7.8 %copy-start = (bf16[10,192,128]{2,1,0:T(8,128)(2,1)S(1)}, bf16[10,192,128]{2,1,0:T(8,128)(2,1)}, u32[]{:S(2)}) copy-start(bf16[10,192,128]{2,1,0:T(8,128)(2,1)} %stage.1.refs_0_.refs_5_) | copy-start | bytes 1474564
  17.9 19.6 %all-to-all-start.1 = ((bf16[16,5,16,128]{3,2,1,0:T(8,128)(2,1)}), bf16[16,5,16,128]{3,2,1,0:T(8,128)(2,1)S(1)}, u32[]{:S(2)}, u32[]{:S(2)}) async-start(bf16[16,5,16,128]{3,2,1,0:T(8,128)(2,1)} %spread.1), calls=%async_computation.1 | async-start | bytes 655360 | tf_op jit(solution)/shard_map/all_to_all | solution.py:472
  36.7 0.8 %copy-start.2 = (bf16[1024,256]{1,0:T(8,128)(2,1)}, bf16[1024,256]{1,0:T(8,128)(2,1)S(1)}, u32[]{:S(2)}) copy-start(bf16[1024,256]{1,0:T(8,128)(2,1)S(1)} %get-tuple-element.16.refs_4_) | copy-start | bytes 1572868
  37.5 0.7 copy-start.1
  38.1 1.0 %copy-start.3 = (bf16[1024,256]{1,0:T(8,128)(2,1)S(1)}, bf16[1024,256]{1,0:T(8,128)(2,1)}, u32[]{:S(2)}) copy-start(bf16[1024,256]{1,0:T(8,128)(2,1)} %copy-done.2) | copy-start | bytes 1572868

commit v3 on v2

--- a/solution.py
+++ b/solution.py
@@ -62,11 +62,10 @@
                 d[128 * h + 32 * k : 128 * h + 32 * k + 32, :] = tile.astype(BF)
 
 
-def build_tables(held, t1, t2, t3, t4, t6):
-    w2, w3, w4, w6 = taps_of(held, 0, 32), taps_of(held, 32, 64), taps_of(held, 64, 128), taps_of(held, 160, 192)
+def build_tables(held, t1, t2, t3, t4):
+    w2, w3, w4 = taps_of(held, 0, 32), taps_of(held, 32, 64), taps_of(held, 64, 128)
 
     fine(w2, 0, 32, 0, [t2.at[0:768]], [], [t2.at[768:1024]])
-    fine(w6, 0, 32, 0, [t6.at[0:768]], [], [t6.at[768:1024]])
 
     row, lane = iota((16, 256), 0), iota((16, 256), 1) // 32
     first = spread(held[9, 0:16, 0:32], 8, False)
@@ -102,8 +101,9 @@
         t4[1, 768 + 64 * s : 832 + 64 * s, :] = jnp.where(edge == 0, g[s], 0.0).astype(BF)
 
 
-def build_join(held, t5, th):
-    w5 = taps_of(held, 128, 160)
+def build_join(held, t5, t6, th):
+    w5, w6 = taps_of(held, 128, 160), taps_of(held, 160, 192)
+    fine(w6, 0, 32, 0, [t6.at[0:768]], [], [t6.at[768:1024]])
     fine(w5, 64, 96, 1280, [t5.at[q, h] for q in range(2) for h in range(2)], [t5.at[0], t5.at[1]], [])
 
     row, lane = iota((256, 256), 0) // 64, iota((256, 256), 1) // 32
@@ -159,8 +159,8 @@
     return taps + [wo[None, :]]
 
 
-TABLES = [(2, 48, 256), (1024, 256), (768, 512), (2, 960, 256), (1024, 256)]
-JOIN = [(2, 2, 1504, 256), (512, 128)]
+TABLES = [(2, 48, 256), (1024, 256), (768, 512), (2, 960, 256)]
+JOIN = [(2, 2, 1504, 256), (1024, 256), (512, 128)]
 
 
 def network(edges, n, wh, p, l1, a1, a2, pool, m1, m2, d1, weights, emit):
@@ -312,8 +312,8 @@
 
 
 def xz_kernel(edges, v, *refs):
-    held, out, tables, (vf, pf, hx), join, scratch = refs[0], refs[1], refs[2:7], refs[7:10], refs[10:12], refs[12:]
-    weights = (*tables[:4], join[0], tables[4], join[1])
+    held, out, tables, (vf, pf, hx), join, scratch = refs[0], refs[1], refs[2:6], refs[6:9], refs[9:12], refs[12:]
+    weights = (*tables, *join)
     n, wh = 16, 32
     for z in range(16):
         vf[16 * z : 16 * z + 16, :] = v[z].astype(F32)
@@ -358,9 +358,9 @@
         out[p, 4] = row[...]
 
 
-def yz_kernel(edges, xflags, v, shared, xz, *refs):
-    tables, held, (out, vf, hf, hy, rf), join, scratch = refs[:5], refs[5], refs[6:11], refs[11:13], refs[13:]
-    weights = (*tables[:4], join[0], tables[4], join[1])
+def yz_kernel(edges, v, shared, xz, *refs):
+    tables, held, (out, vf, hf, hy, rf), join, scratch = refs[:4], refs[4], refs[5:10], refs[10:13], refs[13:]
+    weights = (*tables, *join)
     build_join(held, *join)
     n, wh = 64, 8
     p = scratch[0]
@@ -395,7 +395,7 @@
         yz = jnp.transpose(hy[64 * y : 64 * y + 64, :])[0:16, :]
         yz = jnp.where(yes, plane + yz, plane).astype(BF).astype(F32)
         xz_new = (plane + xz[y]).astype(BF).astype(F32)
-        xz_new = jnp.where(xflags[y] > 0, xz_new, plane)
+        xz_new = jnp.where(edges[4 + y] > 0, xz_new, plane)
         rf[pl.ds(y, 16, stride=16), 0:64] = 0.5 * (xz_new + yz)
     for z in range(16):
         block = rf[16 * z : 16 * z + 16, 0:64].astype(BF)
@@ -414,12 +414,12 @@
                     out[s, z] = rolled[:, 128 * s : 128 * s + 128]
 
 
-def compute(xz_edges, yz_edges, xz_tissue, v, shared, raw):
+def compute(xz_edges, yz_edges, v, shared, raw):
     xz, *tables = pl.pallas_call(
         xz_kernel,
         out_shape=[jax.ShapeDtypeStruct((16, 16, 64), F32)] + [jax.ShapeDtypeStruct(s, BF) for s in TABLES],
         in_specs=[SMEM, VMEM, VMEM],
-        out_specs=[VMEM] * 6,
+        out_specs=[VMEM] * 5,
         scratch_shapes=[pltpu.VMEM((256, 128), F32), pltpu.VMEM((1280, 128), F32), pltpu.VMEM((1024, 128), F32)]
         + [pltpu.VMEM(s, BF) for s in JOIN]
         + unet_scratch(16, 32),
@@ -430,7 +430,7 @@
     return pl.pallas_call(
         yz_kernel,
         out_shape=jax.ShapeDtypeStruct((16, 2, 16, 64), BF),
-        in_specs=[SMEM, SMEM] + [VMEM] * 9,
+        in_specs=[SMEM] + [VMEM] * 8,
         out_specs=VMEM,
         scratch_shapes=[
             pltpu.VMEM((256, 128), F32),
@@ -443,7 +443,7 @@
         compiler_params=pltpu.CompilerParams(vmem_limit_bytes=24 << 20),
         cost_estimate=pl.CostEstimate(flops=6_000_000_000, bytes_accessed=6_000_000, transcendentals=0),
         name="yz",
-    )(yz_edges, xz_tissue, v, shared, xz, *tables, raw)
+    )(yz_edges, v, shared, xz, *tables, raw)
 
 
 def per_device(volume, xz_tissue, yz_tissue, *weights):
@@ -474,8 +474,9 @@
     window = 2 * slab + ch
     xz_edges = jnp.stack([window == 0, window == 15]).astype(jnp.int32)
     yz_edges = jnp.stack([tile == 0, tile == 15, tile, ch]).astype(jnp.int32)
-
-    block = compute(xz_edges, yz_edges, xz_tissue, v, shared, raw)
+    yz_edges = jnp.concatenate([yz_edges, xz_tissue])
+
+    block = compute(xz_edges, yz_edges, v, shared, raw)
     back = lax.all_to_all(block, ("slab", "ch"), split_axis=0, concat_axis=0, tiled=True)
     return jnp.transpose(back, (1, 2, 0, 3)).reshape(2, 16, 1024)
 

time: 66.6 us -> 64.1 us (0.962)
  local copies, waits for them, and re-layouts: 4.35 us -> 2.58 us
  waiting for transfers between devices: 4.37 us -> 3.7 us
    unnamed x12 -> x8, local copies, waits for them, and re-layouts: 3.43 us -> 1.58 us
    all_to_all x1, waiting for transfers between devices: 4.37 us -> 3.69 us  [per_device(): lax.all_to_all(packed, 'slab', split_axis=0, concat_axis=0, tiled=True)]
  transfers between devices with their start and end apart: 2 -> 2, of which waited for: 1 -> 1; matrix products, arithmetic and copies ran while one was open for 0% -> 0% of each run, Pallas kernels for 21% -> 22%
where the time goes in v3:
time: 64.1 us; the launch traced here: 63.2 us
  Pallas kernels  28.8 us (45%)
  starting transfers between devices  15 us (23%)
  blocking collectives  12.9 us (20%)
  waiting for transfers between devices  3.7 us (6%)
  local copies, waits for them, and re-layouts  2.58 us (4%)
    all_to_all x1, blocking collectives, per_device(): lax.all_to_all(block, ('slab', 'ch'), split_axis=0, concat_axis=0, tiled=...  12.9 us
    pallas_call x1, Pallas kernels, compute(): pl.pallas_call(yz_kernel, out_shape=jax.ShapeDtypeStruct((16, 2, 16, 64),...  12.5 us
    pallas_call x1, Pallas kernels, compute(): pl.pallas_call(xz_kernel, out_shape=[jax.ShapeDtypeStruct((16, 16, 64), F...  11.9 us
    all_to_all x1, starting transfers between devices, per_device(): lax.all_to_all(packed, 'slab', split_axis=0, concat_axis=0, tiled=True)  8.19 us
    all_to_all x1, starting transfers between devices, per_device(): lax.all_to_all(shared, 'tile', split_axis=0, concat_axis=0, tiled=True)  6.83 us
    all_to_all x1, waiting for transfers between devices, per_device(): lax.all_to_all(packed, 'slab', split_axis=0, concat_axis=0, tiled=True)  3.69 us
    pallas_call x1, Pallas kernels, stage(): pl.pallas_call(stage_kernel, out_shape=jax.ShapeDtypeStruct((10, 192, 128...  1.93 us
    unnamed x8, local copies, waits for them, and re-layouts  1.58 us
  transfers between devices with their start and end apart: 2, of which 1 were waited for; matrix products, arithmetic and copies ran while one was open for 0% of the time, Pallas kernels for 22%

profile of v3, /device:TPU:9, one launch (start us, length us, event | category | flops | bytes accessed | tf_op | source)
XLA Modules:
  0.0 63.2 jit_solution(433442833456797046)
XLA Ops:
  0.0 1.6 %pack.1 = bf16[8,2,16,128]{3,2,1,0:T(8,128)(2,1)} custom-call(s32[1]{0:T(128)} %bitcast.3.side, bf16[2,16,1024]{2,1,0:T(8,128)(2,1)} %v.1), custom_call_target="tpu_custom_call" | custom-call | tf_op jit(solution)/shard_map/pack/pallas_call | solution.py:451
  1.6 8.2 %all-to-all-start = ((bf16[8,2,16,128]{3,2,1,0:T(8,128)(2,1)}), bf16[8,2,16,128]{3,2,1,0:T(8,128)(2,1)S(1)}, u32[]{:S(2)}, u32[]{:S(2)}) async-start(bf16[8,2,16,128]{3,2,1,0:T(8,128)(2,1)} %pack.1), calls=%async_computation | async-start | bytes 131072 | tf_op jit(solution)/shard_map/all_to_all | solution.py:458
  9.7 0.0 copy-start.1
  9.7 0.7 %copy-done.1 = s32[8]{0:T(128)S(1)} copy-done((s32[8]{0:T(128)S(1)}, s32[8]{0:T(128)}, u32[]{:S(2)}) %copy-start.1) | copy-done | bytes 56
  10.4 0.1 broadcast_in_dim_tile.3
  10.5 0.0 copy-start.2
  10.5 0.6 %copy-done.2 = s32[16]{0:T(128)S(1)} copy-done((s32[16]{0:T(128)S(1)}, s32[16]{0:T(128)}, u32[]{:S(2)}) %copy-start.2) | copy-done | bytes 88
  11.2 0.1 concatenate.3.edges
  11.3 1.9 %stage.1.refs_0_.refs_4_ = bf16[10,192,128]{2,1,0:T(8,128)(2,1)} custom-call(bf16[9,32]{1,0:T(8,128)(2,1)} %bitcast.28, bf16[9,32,32]{2,1,0:T(8,128)(2,1)} %bitcast.24, bf16[9,32,64]{2,1,0:T(8,128)(2,1)} %bitcast.25, bf16[9,64,64]{2,1,0:T(8,128)(2,1)} %bitcast.23, bf16[9,32,96]{2,1,0:T(8,128)(2,1)} %bitcast.26, bf16[9,32,32]{2,1,0:T(8,128)(2,1)} %bitcast.27, ...), custom_call_target="tpu_custom_call" | custom-call | tf_op jit(solution)/shard_map/stage/pallas_call | solution.py:147
  13.2 0.1 add_convert_fusion.edges
  13.3 3.7 %all-to-all-done = bf16[8,2,16,128]{3,2,1,0:T(8,128)(2,1)S(1)} async-done(((bf16[8,2,16,128]{3,2,1,0:T(8,128)(2,1)}), bf16[8,2,16,128]{3,2,1,0:T(8,128)(2,1)S(1)}, u32[]{:S(2)}, u32[]{:S(2)}) %all-to-all-start) | async-done | bytes 65568 | tf_op jit(solution)/shard_map/all_to_all | solution.py:458
  17.0 0.0 copy-start
  17.0 0.9 %spread.1 = bf16[16,5,16,128]{3,2,1,0:T(8,128)(2,1)} custom-call(s32[1]{0:T(128)} %bitcast.2.place, bf16[16,16,128]{2,1,0:T(8,128)(2,1)S(1)} %bitcast.19, bf16[16,128]{1,0:T(8,128)(2,1)S(1)} %broadcast_in_dim.6.row), custom_call_target="tpu_custom_call" | custom-call | tf_op jit(solution)/shard_map/spread/pallas_call | solution.py:464
  17.9 6.8 %all-to-all-start.1 = ((bf16[16,5,16,128]{3,2,1,0:T(8,128)(2,1)}), bf16[16,5,16,128]{3,2,1,0:T(8,128)(2,1)S(1)}, u32[]{:S(2)}, u32[]{:S(2)}) async-start(bf16[16,5,16,128]{3,2,1,0:T(8,128)(2,1)} %spread.1), calls=%async_computation.1 | async-start | bytes 655360 | tf_op jit(solution)/shard_map/all_to_all | solution.py:472
  24.7 0.0 copy-done
  24.7 11.9 %xz.1 = (f32[16,16,64]{2,1,0:T(8,128)S(1)}, bf16[2,48,256]{2,1,0:T(8,128)(2,1)S(1)}, bf16[1024,256]{1,0:T(8,128)(2,1)S(1)}, bf16[768,512]{1,0:T(8,128)(2,1)S(1)}, bf16[2,960,256]{2,1,0:T(8,128)(2,1)S(1)}) custom-call(s32[2]{0:T(128)S(1)} %add_convert_fusion.edges, bf16[16,16,128]{2,1,0:T(8,128)(2,1)S(1)} %bitcast.20, bf16[10,192,128]{2,1,0:T(8,128)(2,1)S(1)} %copy-done), custom_call_target="tpu_custom_call" | custom-call | flops 6000000000 | bytes 6000000 | tf_op jit(solution)/shard_map/xz/pallas_call | solution.py:418
  36.6 0.0 all-to-all-done.1.shared
  36.6 12.5 %yz.1 = bf16[16,2,16,64]{3,2,1,0:T(8,128)(2,1)S(1)} custom-call(s32[20]{0:T(128)S(1)} %concatenate.3.edges, bf16[16,16,128]{2,1,0:T(8,128)(2,1)S(1)} %bitcast.21, bf16[16,5,16,128]{3,2,1,0:T(8,128)(2,1)S(1)} %all-to-all-done.1.shared, f32[16,16,64]{2,1,0:T(8,128)S(1)} %get-tuple-element.10.xz, bf16[2,48,256]{2,1,0:T(8,128)(2,1)S(1)} %get-tuple-element.11.refs_0_, ...), custom_call_target="tpu_custom_call" | custom-call | flops 6000000000 | bytes 6000000 | tf_op jit(solution)/shard_map/yz/pallas_call | solution.py:430
  49.2 0.1 reshape.34
  49.3 12.9 %all_to_all.15 = bf16[16,2,1024]{2,1,0:T(2,128)(2,1)S(1)} all-to-all(bf16[16,2,1024]{2,1,0:T(2,128)(2,1)S(1)} %reshape.34), channel_id=1, replica_groups=mesh['slab'=8,'tile'=16,'ch'=2] {'slab','ch'}, dimensions={0} | all-to-all | bytes 131072 | tf_op jit(solution)/shard_map/all_to_all | solution.py:480
  62.2 0.1 reshape.35
  62.3 0.1 copy.11
  62.4 0.8 %reshape.31 = bf16[2,16,1024]{2,1,0:T(8,128)(2,1)} reshape(bf16[2,16,16,64]{3,2,1,0:T(8,128)(2,1)S(1)} %copy.11) | data formatting | bytes 131072 | tf_op jit(solution)/shard_map/reshape | solution.py:481
  (3 shorter events, 0.0 us)
Async XLA Ops:
  1.6 15.4 %all-to-all-start = ((bf16[8,2,16,128]{3,2,1,0:T(8,128)(2,1)}), bf16[8,2,16,128]{3,2,1,0:T(8,128)(2,1)S(1)}, u32[]{:S(2)}, u32[]{:S(2)}) async-start(bf16[8,2,16,128]{3,2,1,0:T(8,128)(2,1)} %pack.1), calls=%async_computation | async-start | bytes 131072 | tf_op jit(solution)/shard_map/all_to_all | solution.py:458
  9.7 0.7 %copy-start.1 = (s32[8]{0:T(128)S(1)}, s32[8]{0:T(128)}, u32[]{:S(2)}) copy-start(s32[8]{0:T(128)} %param.12) | copy-start | bytes 100
  10.5 0.7 %copy-start.2 = (s32[16]{0:T(128)S(1)}, s32[16]{0:T(128)}, u32[]{:S(2)}) copy-start(s32[16]{0:T(128)} %param.11) | copy-start | bytes 196
  17.0 7.8 %copy-start = (bf16[10,192,128]{2,1,0:T(8,128)(2,1)S(1)}, bf16[10,192,128]{2,1,0:T(8,128)(2,1)}, u32[]{:S(2)}) copy-start(bf16[10,192,128]{2,1,0:T(8,128)(2,1)} %stage.1.refs_0_.refs_4_) | copy-start | bytes 1474564
  17.9 18.7 %all-to-all-start.1 = ((bf16[16,5,16,128]{3,2,1,0:T(8,128)(2,1)}), bf16[16,5,16,128]{3,2,1,0:T(8,128)(2,1)S(1)}, u32[]{:S(2)}, u32[]{:S(2)}) async-start(bf16[16,5,16,128]{3,2,1,0:T(8,128)(2,1)} %spread.1), calls=%async_computation.1 | async-start | bytes 655360 | tf_op jit(solution)/shard_map/all_to_all | solution.py:472

commit v4 on v3

--- a/solution.py
+++ b/solution.py
@@ -359,10 +359,10 @@
 
 
 def yz_kernel(edges, v, shared, xz, *refs):
-    tables, held, (out, vf, hf, hy, rf), join, scratch = refs[:4], refs[4], refs[5:10], refs[10:13], refs[13:]
+    tables, held, (out, vf, hf, hy, rf, vc, hc, oc), join, scratch = refs[:4], refs[4], refs[5:13], refs[13:16], refs[16:]
     weights = (*tables, *join)
     build_join(held, *join)
-    n, wh = 64, 8
+    wh = 8
     p = scratch[0]
     tile, octet = edges[2], 8 * edges[3]
     for z in range(16):
@@ -373,27 +373,52 @@
             for i in range(2):
                 at = 16 * (2 * k + i) + 8 * side
                 hf[at : at + 8, :] = both[8 * i : 8 * i + 8, :]
-    for k in range(32):
-        at = slice(n * (k // 2), n * (k // 2) + n)
-        if 8 <= k < 24:
-            turned = jnp.transpose(vf[pl.ds(k - 8, 16, stride=16), :])
-            p[k % 2, at, :] = turned[HALO : HALO + n, :].astype(BF)
-        else:
-            turned = jnp.transpose(hf[pl.ds(k if k < 8 else k - 16, 8, stride=16), :])
-            p[k % 2, at, :] = jnp.concatenate([turned[0:n, :], turned[n:, :]], axis=1).astype(BF)
-
-    def emit(q, j0, cols, head):
-        for k in range(cols):
-            at = pl.multiple_of((2 * (j0 + k) + q) * n, 16)
-            hy[pl.ds(at, n), :] = head[k * n : k * n + n, :]
-
-    network(edges, n, wh, *scratch, weights, emit)
-
-    yes = sum(shared[octet + i, 4].astype(F32) for i in range(8))[0:1, 0:64] > 0.5
+
+    flags = sum(shared[octet + i, 4].astype(F32) for i in range(8))
+    square = (128, 128)
+    earlier = (iota(square, 0) < iota(square, 1)).astype(F32).astype(BF)
+    rank = dot(flags.astype(BF), earlier)[0:1].astype(jnp.int32)
+    yes = flags[0:1] > 0.5
+    spots = jnp.where((iota(square, 0) == rank) & yes, 1.0, 0.0)
+    back = jnp.transpose(spots)
+    twice = back + pltpu.roll(pltpu.roll(back, 64, 0), 64, 1)
+    vc[...] = dot(vf[...].astype(BF), pltpu.roll(back, HALO, 0).astype(BF))
+    hc[...] = dot(hf[...].astype(BF), twice.astype(BF))
+    count = jnp.sum(flags[0:1]).astype(jnp.int32)
+    oc[...] = jnp.zeros_like(oc)
+
+    def run(n):
+        for k in range(32):
+            at = slice(n * (k // 2), n * (k // 2) + n)
+            if 8 <= k < 24:
+                turned = jnp.transpose(vc[pl.ds(k - 8, 16, stride=16), :])
+                p[k % 2, at, :] = turned[0:n, :].astype(BF)
+            else:
+                turned = jnp.transpose(hc[pl.ds(k if k < 8 else k - 16, 8, stride=16), :])
+                p[k % 2, at, :] = jnp.concatenate([turned[0:n, :], turned[64 : 64 + n, :]], axis=1).astype(BF)
+
+        def emit(q, j0, cols, head):
+            for k in range(cols):
+                at = pl.multiple_of((2 * (j0 + k) + q) * n, 16)
+                hy[pl.ds(at, n), :] = head[k * n : k * n + n, :]
+
+        network(edges, n, wh, *scratch, weights, emit)
+        for y in range(16):
+            plane = vc[pl.ds(y, 16, stride=16), :][:, 0:n]
+            new = plane + jnp.transpose(hy[n * y : n * y + n, :])[0:16, :]
+            oc[16 * y : 16 * y + 16, 0:n] = new.astype(BF)
+
+    for n, low in ((32, -1), (48, 32), (64, 48)):
+
+        @pl.when((count > low) & (count <= (32 if low < 0 else low + 16)))
+        def _(n=n):
+            run(n)
+
+    spread = dot(oc[...], spots.astype(BF))
+    yes = yes[:, 0:64]
     for y in range(16):
         plane = pltpu.roll(vf[pl.ds(y, 16, stride=16), :], 128 - HALO, 1)[:, 0:64]
-        yz = jnp.transpose(hy[64 * y : 64 * y + 64, :])[0:16, :]
-        yz = jnp.where(yes, plane + yz, plane).astype(BF).astype(F32)
+        yz = jnp.where(yes, spread[16 * y : 16 * y + 16, 0:64], plane)
         xz_new = (plane + xz[y]).astype(BF).astype(F32)
         xz_new = jnp.where(edges[4 + y] > 0, xz_new, plane)
         rf[pl.ds(y, 16, stride=16), 0:64] = 0.5 * (xz_new + yz)
@@ -437,6 +462,9 @@
             pltpu.VMEM((128, 128), F32),
             pltpu.VMEM((1024, 128), F32),
             pltpu.VMEM((256, 128), F32),
+            pltpu.VMEM((256, 128), F32),
+            pltpu.VMEM((128, 128), F32),
+            pltpu.VMEM((256, 128), BF),
         ]
         + [pltpu.VMEM(s, BF) for s in JOIN]
         + unet_scratch(64, 8),

time: 64.1 us -> 62.5 us (0.975)
  Pallas kernels: 28.8 us -> 25.8 us
  blocking collectives: 12.9 us -> 14.4 us
    pallas_call x1, Pallas kernels: 12.5 us -> 9.48 us  [compute(): pl.pallas_call(yz_kernel, out_shape=jax.ShapeDtypeStruct((16, 2, 16, 64),...]
    all_to_all x1, blocking collectives: 12.9 us -> 14.4 us  [per_device(): lax.all_to_all(block, ('slab', 'ch'), split_axis=0, concat_axis=0, tiled=...]
where the time goes in v4:
time: 62.5 us; the launch traced here: 61.6 us
  Pallas kernels  25.8 us (41%)
  starting transfers between devices  15 us (24%)
  blocking collectives  14.4 us (23%)
  waiting for transfers between devices  3.7 us (6%)
  local copies, waits for them, and re-layouts  2.58 us (4%)
    all_to_all x1, blocking collectives, per_device(): lax.all_to_all(block, ('slab', 'ch'), split_axis=0, concat_axis=0, tiled=...  14.4 us
    pallas_call x1, Pallas kernels, compute(): pl.pallas_call(xz_kernel, out_shape=[jax.ShapeDtypeStruct((16, 16, 64), F...  11.9 us
    pallas_call x1, Pallas kernels, compute(): pl.pallas_call(yz_kernel, out_shape=jax.ShapeDtypeStruct((16, 2, 16, 64),...  9.48 us
    all_to_all x1, starting transfers between devices, per_device(): lax.all_to_all(packed, 'slab', split_axis=0, concat_axis=0, tiled=True)  8.19 us
    all_to_all x1, starting transfers between devices, per_device(): lax.all_to_all(shared, 'tile', split_axis=0, concat_axis=0, tiled=True)  6.83 us
    all_to_all x1, waiting for transfers between devices, per_device(): lax.all_to_all(packed, 'slab', split_axis=0, concat_axis=0, tiled=True)  3.69 us
    pallas_call x1, Pallas kernels, stage(): pl.pallas_call(stage_kernel, out_shape=jax.ShapeDtypeStruct((10, 192, 128...  1.93 us
    unnamed x8, local copies, waits for them, and re-layouts  1.58 us
  transfers between devices with their start and end apart: 2, of which 1 were waited for; matrix products, arithmetic and copies ran while one was open for 0% of the time, Pallas kernels for 22%

profile of v4, /device:TPU:9, one launch (start us, length us, event | category | flops | bytes accessed | tf_op | source)
XLA Modules:
  0.0 61.6 jit_solution(5981759707930225776)
XLA Ops:
  0.0 1.6 %pack.1 = bf16[8,2,16,128]{3,2,1,0:T(8,128)(2,1)} custom-call(s32[1]{0:T(128)} %bitcast.3.side, bf16[2,16,1024]{2,1,0:T(8,128)(2,1)} %v.1), custom_call_target="tpu_custom_call" | custom-call | tf_op jit(solution)/shard_map/pack/pallas_call | solution.py:479
  1.6 8.2 %all-to-all-start = ((bf16[8,2,16,128]{3,2,1,0:T(8,128)(2,1)}), bf16[8,2,16,128]{3,2,1,0:T(8,128)(2,1)S(1)}, u32[]{:S(2)}, u32[]{:S(2)}) async-start(bf16[8,2,16,128]{3,2,1,0:T(8,128)(2,1)} %pack.1), calls=%async_computation | async-start | bytes 131072 | tf_op jit(solution)/shard_map/all_to_all | solution.py:486
  9.7 0.0 copy-start.1
  9.7 0.7 %copy-done.1 = s32[8]{0:T(128)S(1)} copy-done((s32[8]{0:T(128)S(1)}, s32[8]{0:T(128)}, u32[]{:S(2)}) %copy-start.1) | copy-done | bytes 56
  10.4 0.1 broadcast_in_dim_tile.3
  10.5 0.0 copy-start.2
  10.5 0.6 %copy-done.2 = s32[16]{0:T(128)S(1)} copy-done((s32[16]{0:T(128)S(1)}, s32[16]{0:T(128)}, u32[]{:S(2)}) %copy-start.2) | copy-done | bytes 88
  11.2 0.1 concatenate.3.edges
  11.3 1.9 %stage.1.refs_0_.refs_4_ = bf16[10,192,128]{2,1,0:T(8,128)(2,1)} custom-call(bf16[9,32]{1,0:T(8,128)(2,1)} %bitcast.28, bf16[9,32,32]{2,1,0:T(8,128)(2,1)} %bitcast.24, bf16[9,32,64]{2,1,0:T(8,128)(2,1)} %bitcast.25, bf16[9,64,64]{2,1,0:T(8,128)(2,1)} %bitcast.23, bf16[9,32,96]{2,1,0:T(8,128)(2,1)} %bitcast.26, bf16[9,32,32]{2,1,0:T(8,128)(2,1)} %bitcast.27, ...), custom_call_target="tpu_custom_call" | custom-call | tf_op jit(solution)/shard_map/stage/pallas_call | solution.py:147
  13.2 0.1 add_convert_fusion.edges
  13.3 3.7 %all-to-all-done = bf16[8,2,16,128]{3,2,1,0:T(8,128)(2,1)S(1)} async-done(((bf16[8,2,16,128]{3,2,1,0:T(8,128)(2,1)}), bf16[8,2,16,128]{3,2,1,0:T(8,128)(2,1)S(1)}, u32[]{:S(2)}, u32[]{:S(2)}) %all-to-all-start) | async-done | bytes 65568 | tf_op jit(solution)/shard_map/all_to_all | solution.py:486
  17.0 0.0 copy-start
  17.0 0.9 %spread.1 = bf16[16,5,16,128]{3,2,1,0:T(8,128)(2,1)} custom-call(s32[1]{0:T(128)} %bitcast.2.place, bf16[16,16,128]{2,1,0:T(8,128)(2,1)S(1)} %bitcast.19, bf16[16,128]{1,0:T(8,128)(2,1)S(1)} %broadcast_in_dim.6.row), custom_call_target="tpu_custom_call" | custom-call | tf_op jit(solution)/shard_map/spread/pallas_call | solution.py:492
  17.9 6.8 %all-to-all-start.1 = ((bf16[16,5,16,128]{3,2,1,0:T(8,128)(2,1)}), bf16[16,5,16,128]{3,2,1,0:T(8,128)(2,1)S(1)}, u32[]{:S(2)}, u32[]{:S(2)}) async-start(bf16[16,5,16,128]{3,2,1,0:T(8,128)(2,1)} %spread.1), calls=%async_computation.1 | async-start | bytes 655360 | tf_op jit(solution)/shard_map/all_to_all | solution.py:500
  24.7 0.0 copy-done
  24.7 11.9 %xz.1 = (f32[16,16,64]{2,1,0:T(8,128)S(1)}, bf16[2,48,256]{2,1,0:T(8,128)(2,1)S(1)}, bf16[1024,256]{1,0:T(8,128)(2,1)S(1)}, bf16[768,512]{1,0:T(8,128)(2,1)S(1)}, bf16[2,960,256]{2,1,0:T(8,128)(2,1)S(1)}) custom-call(s32[2]{0:T(128)S(1)} %add_convert_fusion.edges, bf16[16,16,128]{2,1,0:T(8,128)(2,1)S(1)} %bitcast.20, bf16[10,192,128]{2,1,0:T(8,128)(2,1)S(1)} %copy-done), custom_call_target="tpu_custom_call" | custom-call | flops 6000000000 | bytes 6000000 | tf_op jit(solution)/shard_map/xz/pallas_call | solution.py:443
  36.6 0.0 all-to-all-done.1.shared
  36.6 9.5 %yz.1 = bf16[16,2,16,64]{3,2,1,0:T(8,128)(2,1)S(1)} custom-call(s32[20]{0:T(128)S(1)} %concatenate.3.edges, bf16[16,16,128]{2,1,0:T(8,128)(2,1)S(1)} %bitcast.21, bf16[16,5,16,128]{3,2,1,0:T(8,128)(2,1)S(1)} %all-to-all-done.1.shared, f32[16,16,64]{2,1,0:T(8,128)S(1)} %get-tuple-element.10.xz, bf16[2,48,256]{2,1,0:T(8,128)(2,1)S(1)} %get-tuple-element.11.refs_0_, ...), custom_call_target="tpu_custom_call" | custom-call | flops 6000000000 | bytes 6000000 | tf_op jit(solution)/shard_map/yz/pallas_call | solution.py:455
  46.1 0.1 reshape.34
  46.3 14.4 %all_to_all.15 = bf16[16,2,1024]{2,1,0:T(2,128)(2,1)S(1)} all-to-all(bf16[16,2,1024]{2,1,0:T(2,128)(2,1)S(1)} %reshape.34), channel_id=1, replica_groups=mesh['slab'=8,'tile'=16,'ch'=2] {'slab','ch'}, dimensions={0} | all-to-all | bytes 131072 | tf_op jit(solution)/shard_map/all_to_all | solution.py:508
  60.6 0.1 reshape.35
  60.8 0.1 copy.11
  60.8 0.8 %reshape.31 = bf16[2,16,1024]{2,1,0:T(8,128)(2,1)} reshape(bf16[2,16,16,64]{3,2,1,0:T(8,128)(2,1)S(1)} %copy.11) | data formatting | bytes 131072 | tf_op jit(solution)/shard_map/reshape | solution.py:509
  (3 shorter events, 0.0 us)
Async XLA Ops:
  1.6 15.4 %all-to-all-start = ((bf16[8,2,16,128]{3,2,1,0:T(8,128)(2,1)}), bf16[8,2,16,128]{3,2,1,0:T(8,128)(2,1)S(1)}, u32[]{:S(2)}, u32[]{:S(2)}) async-start(bf16[8,2,16,128]{3,2,1,0:T(8,128)(2,1)} %pack.1), calls=%async_computation | async-start | bytes 131072 | tf_op jit(solution)/shard_map/all_to_all | solution.py:486
  9.7 0.7 %copy-start.1 = (s32[8]{0:T(128)S(1)}, s32[8]{0:T(128)}, u32[]{:S(2)}) copy-start(s32[8]{0:T(128)} %param.12) | copy-start | bytes 100
  10.5 0.7 %copy-start.2 = (s32[16]{0:T(128)S(1)}, s32[16]{0:T(128)}, u32[]{:S(2)}) copy-start(s32[16]{0:T(128)} %param.11) | copy-start | bytes 196
  17.0 7.8 %copy-start = (bf16[10,192,128]{2,1,0:T(8,128)(2,1)S(1)}, bf16[10,192,128]{2,1,0:T(8,128)(2,1)}, u32[]{:S(2)}) copy-start(bf16[10,192,128]{2,1,0:T(8,128)(2,1)} %stage.1.refs_0_.refs_4_) | copy-start | bytes 1474564
  17.9 18.7 %all-to-all-start.1 = ((bf16[16,5,16,128]{3,2,1,0:T(8,128)(2,1)}), bf16[16,5,16,128]{3,2,1,0:T(8,128)(2,1)S(1)}, u32[]{:S(2)}, u32[]{:S(2)}) async-start(bf16[16,5,16,128]{3,2,1,0:T(8,128)(2,1)} %spread.1), calls=%async_computation.1 | async-start | bytes 655360 | tf_op jit(solution)/shard_map/all_to_all | solution.py:500
